TPU v7x, 256 devices: a whole 4x4x8 slice. The times are simulated.
256 devices in a mesh: dp: 16 (over z_hi, y, core), space: 16 (over x, z_lo).
Axes of the slice: x: 4, y: 4, z: 8 (z_hi: 2, z_lo: 4; z = z_hi * 4 + z_lo), core: 2. Of those that a mesh axis runs over, the one named last changes fastest.
Arguments:
- fields: bfloat16 [16, 128, 128, 512], P('dp', 'space'), may hold values from -6 to 6
- bn_scale: float32 [512], replicated, may hold values from 0.5 to 1.5
- bn_shift: float32 [512], replicated, may hold values from -3 to 3
- w_expand: bfloat16 [512, 2048], P(None, 'dp'), may hold values from -0.25 to 0.25
- expand_bias: float32 [2048], replicated, may hold values from -3 to 3
- dw_kernel: float32 [3, 3, 2048], replicated, may hold values from -2 to 2
- dw_bias: float32 [2048], replicated, may hold values from -3 to 3
- w_project: bfloat16 [2048, 512], P(None, 'dp'), may hold values from -0.125 to 0.125
- ln_gain: float32 [512], replicated, may hold values from 0.5 to 1.5
- ln_bias: float32 [512], replicated, may hold values from -3 to 3
- w_qkv: bfloat16 [512, 1536], P(None, 'dp'), may hold values from -0.25 to 0.25
- w_out: bfloat16 [512, 512], P(None, 'dp'), may hold values from -0.25 to 0.25
Outputs:
- output: bfloat16 [16, 128, 128, 512], P('dp', 'space')
All inputs are finite; a program needn't handle non-finite values.
Results may differ from a plain program's by a relative error of at most 0.0056.
Values may be sent and summed in bfloat16 or wider, within the bound.
A program may use at most 64 MiB of HBM per device.

v0:
```python
import jax
import jax.numpy as jnp
from jax import lax
from jax.sharding import PartitionSpec as P

HD = 32
GRID = 8
HEIGHT = 128


def padded_2(cells, sides, width):
    for axis, dim in sides:
        count = lax.axis_size(axis)
        ends = count - 1
        head = lax.slice_in_dim(cells, 0, width, axis=dim)
        tail = lax.slice_in_dim(cells, cells.shape[dim] - width, cells.shape[dim], axis=dim)
        cells = jnp.concatenate(
            [
                lax.ppermute(tail, axis, [(i, (i + 1) % count) for i in range(ends)]),
                cells,
                lax.ppermute(head, axis, [((i + 1) % count, i) for i in range(ends)]),
            ],
            axis=dim,
        )
    return cells


def layer_normed(tokens, ln_gain, ln_bias):
    values = tokens.astype(jnp.float32)
    center = jnp.mean(values, axis=-1, keepdims=True)
    spread = jnp.mean(jnp.square(values - center), axis=-1, keepdims=True)
    return ((values - center) * lax.rsqrt(spread + 1e-05) * ln_gain + ln_bias).astype(jnp.bfloat16)


def expand_tokens(tokens, w_expand, expand_bias):
    flat = tokens.reshape(-1, tokens.shape[-1])
    summed = jnp.dot(
        flat, lax.all_gather(w_expand, "dp", axis=1, tiled=True), preferred_element_type=jnp.float32
    )
    expanded = jax.nn.gelu(summed + expand_bias).astype(jnp.bfloat16)
    return expanded.reshape(tokens.shape[:-1] + (summed.shape[1],))


def depthwise(padded, dw_kernel, dw_bias):
    band_rows = padded.shape[1] - 2
    image_cols = padded.shape[2]
    wide = jnp.pad(padded, ((0, 0), (0, 0), (1, 1), (0, 0)))
    accum = jnp.zeros((padded.shape[0], band_rows, image_cols, padded.shape[3]), jnp.float32)
    for row_off in range(3):
        for col_off in range(3):
            accum = (
                accum
                + wide[:, row_off : row_off + band_rows, col_off : col_off + image_cols].astype(
                    jnp.float32
                )
                * dw_kernel[row_off, col_off]
            )
    return jax.nn.gelu(accum + dw_bias).astype(jnp.bfloat16)


def project_back(spatial, w_project):
    flat = spatial.reshape(-1, spatial.shape[-1])
    return jnp.dot(
        flat,
        lax.all_gather(w_project, "dp", axis=1, tiled=True),
        preferred_element_type=jnp.float32,
    )


def qkv_of(tokens, w_qkv):
    flat = tokens.reshape(-1, tokens.shape[-1])
    summed = jnp.dot(
        flat, lax.all_gather(w_qkv, "dp", axis=1, tiled=True), preferred_element_type=jnp.float32
    )
    return summed.astype(jnp.bfloat16).reshape(tokens.shape[:-1] + (summed.shape[1],))


def out_of(attended, w_out):
    flat = attended.reshape(-1, attended.shape[-1])
    summed = jnp.dot(
        flat, lax.all_gather(w_out, "dp", axis=1, tiled=True), preferred_element_type=jnp.float32
    )
    return summed.reshape(attended.shape[:-1] + (summed.shape[1],))


def to_windows(gridded):
    items, height, grid_count, blocks_here, width = gridded.shape
    stride_rows = height // grid_count
    split = gridded.reshape(items, grid_count, stride_rows, grid_count, blocks_here, width)
    split = split.transpose(0, 2, 4, 1, 3, 5)
    return split.reshape(items * stride_rows * blocks_here, grid_count * grid_count, width)


def from_windows(windows, items, blocks_here):
    width = windows.shape[-1]
    stride_rows = HEIGHT // GRID
    split = windows.reshape(items, stride_rows, blocks_here, GRID, GRID, width)
    split = split.transpose(0, 3, 1, 4, 2, 5)
    return split.reshape(items, HEIGHT, GRID, blocks_here, width)


def attend_windows(queries, keyset, valueset):
    window_count, length, width = queries.shape
    heads = width // HD
    query_heads = queries.reshape(window_count, length, heads, HD)
    key_heads = keyset.reshape(window_count, length, heads, HD)
    value_heads = valueset.reshape(window_count, length, heads, HD)
    scores = jnp.einsum(
        "wqhd,wkhd->whqk", query_heads, key_heads, preferred_element_type=jnp.float32
    ) / jnp.sqrt(jnp.float32(HD))
    exponent = jnp.exp(scores)
    soft_weights = (exponent / jnp.sum(exponent, axis=-1, keepdims=True)).astype(jnp.bfloat16)
    mixed = jnp.einsum(
        "whqk,wkhd->wqhd", soft_weights, value_heads, preferred_element_type=jnp.float32
    )
    return mixed.astype(jnp.bfloat16).reshape(window_count, length, width)


def local(
    fields,
    bn_scale,
    bn_shift,
    w_expand,
    expand_bias,
    dw_kernel,
    dw_bias,
    w_project,
    ln_gain,
    ln_bias,
    w_qkv,
    w_out,
):
    batch_local, band_rows, image_cols, chans = fields.shape
    col_blocks = image_cols // GRID
    normed = (fields.astype(jnp.float32) * bn_scale + bn_shift).astype(jnp.bfloat16)
    rimmed = padded_2(normed, (("space", 1),), 1)
    expanded = expand_tokens(rimmed, w_expand, expand_bias)
    position = lax.axis_index("space") * band_rows - 1 + jnp.arange(band_rows + 2, dtype=jnp.int32)
    inside = (position >= 0) & (position < band_rows * lax.axis_size("space"))
    expanded = jnp.where(inside[None, :, None, None], expanded, jnp.zeros_like(expanded))
    spatial = depthwise(expanded, dw_kernel, dw_bias)
    projected = project_back(spatial, w_project).reshape(fields.shape)
    conv_out = (fields.astype(jnp.float32) + projected).astype(jnp.bfloat16)
    banded_in = conv_out.reshape(batch_local, band_rows, GRID, col_blocks, chans)
    gridded = lax.all_to_all(banded_in, "space", split_axis=3, concat_axis=1, tiled=True)
    triple = qkv_of(layer_normed(gridded, ln_gain, ln_bias), w_qkv)
    blocks_here = gridded.shape[3]
    attended = attend_windows(
        to_windows(triple[..., :chans]),
        to_windows(triple[..., chans : 2 * chans]),
        to_windows(triple[..., 2 * chans :]),
    )
    attended = from_windows(attended, batch_local, blocks_here)
    finished = (gridded.astype(jnp.float32) + out_of(attended, w_out)).astype(jnp.bfloat16)
    banded = lax.all_to_all(finished, "space", split_axis=1, concat_axis=3, tiled=True)
    return banded.reshape(fields.shape)


def solution(mesh):
    in_specs = (
        P("dp", "space", None, None),
        P(),
        P(),
        P(None, "dp"),
        P(),
        P(),
        P(),
        P(None, "dp"),
        P(),
        P(),
        P(None, "dp"),
        P(None, "dp"),
    )
    out_specs = P("dp", "space", None, None)
    return jax.shard_map(local, mesh=mesh, in_specs=in_specs, out_specs=out_specs, check_vma=False)
```

profile of v0, /device:TPU:1, one launch (start us, length us, event | category | flops | bytes accessed | tf_op | source)
XLA Modules:
  0.0 318.1 jit_solution(3100902488653482529)
XLA Ops:
  6.5 0.7 all-gather.4.cloned.1.call-update
  7.3 0.7 all-gather.6.cloned.1.call-update
  8.0 1.5 fusion.28
  9.5 1.3 collective-permute-start.1
  10.8 5.0 %collective-permute-start = (bf16[1,1,128,512]{3,2,1,0:T(8,128)(2,1)S(1)}, bf16[1,1,128,512]{3,2,1,0:T(8,128)(2,1)S(1)}, u32[]{:S(2)}, u32[]{:S(2)}) collective-permute-start(bf16[1,1,128,512]{3,2,1,0:T(8,128)(2,1)S(1)} %get-tuple-element.10), channel_id=1, source_target_pairs={{0,1},{1,2},{2,3},{3,4},{4,5},{5,6},{6,7},{7,8},{8,9},{9,10},{10,1... | collective-permute-start | bytes 393224 | tf_op jit(solution)/shard_map/ppermute | solution.py:19
  15.8 1.1 fusion.55
  16.9 0.8 collective-permute-done
  17.9 59.1 %all-gather.4.cloned.1.call-done = bf16[512,2048]{1,0:T(8,128)(2,1)} async-done(((bf16[512,128]{1,0:T(8,128)(2,1)}), bf16[512,2048]{1,0:T(8,128)(2,1)}) %all-gather.4.cloned.1.call-update) | async-done | bytes 2097168 | tf_op jit(solution)/shard_map/all_gather | solution.py:38
  77.1 6.9 %fusion.7 = bf16[1280,2048]{1,0:T(8,128)(2,1)S(1)} fusion(bf16[1280,512]{1,0:T(8,128)(2,1)S(1)} %bitcast.107, bf16[512,2048]{1,0:T(8,128)(2,1)} %all-gather.4.cloned.1.call-done, f32[2048]{0:T(1024)S(1)} %copy-done.5), kind=kOutput, calls=%fused_computation.9 | convolution fusion | flops 2710568960 | bytes 8658944 | tf_op jit(solution)/shard_map/dot_general | solution.py:37
  84.0 2.7 broadcast_select_fusion
  86.7 51.4 %all-gather.6.cloned.1.call-done = bf16[2048,512]{0,1:T(8,128)(2,1)} async-done(((bf16[2048,32]{0,1:T(8,128)(2,1)}), bf16[2048,512]{0,1:T(8,128)(2,1)}) %all-gather.6.cloned.1.call-update) | async-done | bytes 2097168 | tf_op jit(solution)/shard_map/all_gather | solution.py:65
  138.1 28.1 %fusion.29 = bf16[1,8,128,512]{3,2,1,0:T(8,128)(2,1)S(1)} fusion(bf16[1,8,128,512]{3,2,1,0:T(8,128)(2,1)S(1)} %copy-done.1, bf16[2048,512]{0,1:T(8,128)(2,1)} %all-gather.6.cloned.1.call-done, f32[2048]{0:T(1024)S(1)} %copy-done.6, f32[2048]{0:T(1024)S(1)} %bitcast.116, f32[2048]{0:T(1024)S(1)} %bitcast.117, ...), kind=kOutput, calls=%fused_computation.38 | convolution fusion | flops 2224553984 | bytes 22102016 | tf_op jit(solution)/shard_map/dot_general | solution.py:63
  166.2 1.6 copy.41
  167.8 4.3 %all-to-all-start = ((bf16[1,8,8,16,512]{4,2,1,0,3:T(8,128)(2,1)}), bf16[1,8,8,16,512]{4,2,1,0,3:T(8,128)(2,1)S(1)}, u32[]{:S(2)}, u32[]{:S(2)}) async-start(bf16[1,8,8,16,512]{4,2,1,0,3:T(8,128)(2,1)} %copy.41), calls=%async_computation | async-start | bytes 2097152 | tf_op jit(solution)/shard_map/all_to_all | solution.py:145
  172.1 0.7 all-gather.8.cloned.1.call-update
  172.8 45.3 %all_gather.15 = bf16[512,512]{0,1:T(8,128)(2,1)} all-gather(bf16[512,32]{0,1:T(8,128)(2,1)S(1)} %copy-done.2), channel_id=1, replica_groups=mesh['dp'=16,'space'=16] {'dp'}, dimensions={1}, use_global_device_ids=true | all-gather | bytes 557056 | tf_op jit(solution)/shard_map/all_gather | solution.py:81
  219.8 15.2 %all-gather.8.cloned.1.call-done = bf16[512,1536]{0,1:T(8,128)(2,1)} async-done(((bf16[512,96]{0,1:T(8,128)(2,1)}), bf16[512,1536]{0,1:T(8,128)(2,1)}) %all-gather.8.cloned.1.call-update) | async-done | bytes 1572880 | tf_op jit(solution)/shard_map/all_gather | solution.py:73
  235.0 3.2 %fusion.26 = bf16[1,128,8,1,1536]{4,2,1,3,0:T(8,128)(2,1)S(1)} fusion(bf16[1024,512]{1,0:T(8,128)(2,1)S(1)} %fusion.33, bf16[512,1536]{0,1:T(8,128)(2,1)} %all-gather.8.cloned.1.call-done), kind=kOutput, calls=%fused_computation.33 | convolution fusion | flops 1612185600 | bytes 5767168 | tf_op jit(solution)/shard_map/dot_general | solution.py:72
  238.3 1.5 fusion.53
  239.9 3.8 %reshape_reshape.15 = bf16[16,64,16,32]{3,2,1,0:T(8,128)(2,1)} reshape(bf16[1,16,1,8,8,512]{5,4,3,1,2,0:T(8,128)(2,1)S(1)} %copy.46) | data formatting | bytes 2097152 | tf_op jit(solution)/shard_map/reshape;reshape | solution.py:106
  243.7 1.3 copy.45
  245.0 3.8 %reshape_reshape.14 = bf16[16,64,16,32]{3,2,1,0:T(8,128)(2,1)} reshape(bf16[1,16,1,8,8,512]{5,4,3,1,2,0:T(8,128)(2,1)S(1)} %copy.45) | data formatting | bytes 2097152 | tf_op jit(solution)/shard_map/reshape;reshape | solution.py:105
  248.9 1.3 copy.44
  250.2 3.9 %reshape_reshape.13 = bf16[16,64,16,32]{3,2,1,0:T(8,128)(2,1)} reshape(bf16[1,16,1,8,8,512]{5,4,3,1,2,0:T(8,128)(2,1)S(1)} %copy.44) | data formatting | bytes 2097152 | tf_op jit(solution)/shard_map/reshape;reshape | solution.py:107
  254.1 6.5 %fusion.16 = (f32[16,16,64]{2,1,0:T(8,128)S(1)}, f32[16,16,64,64]{2,3,1,0:T(8,128)S(1)}) fusion(bf16[16,64,16,32]{3,2,1,0:T(8,128)(2,1)} %reshape_reshape.15, bf16[16,64,16,32]{3,2,1,0:T(8,128)(2,1)} %reshape_reshape.14), kind=kOutput, calls=%fused_computation.20 | convolution fusion | flops 69189632 | bytes 6356992 | tf_op jit(solution)/shard_map/wqhd,wkhd->whqk/dot_general | solution.py:108
  260.6 3.1 convert_bitcast_fusion
  263.7 5.7 %copy.51 = bf16[16,64,16,32]{3,2,1,0:T(8,128)(2,1)} copy(bf16[16,64,16,32]{1,3,2,0:T(8,128)(2,1)} %convert_bitcast_fusion) | data formatting | bytes 2097152 | tf_op jit(solution)/shard_map/convert_element_type | solution.py:116
  269.4 5.9 %reshape_reshape.16 = bf16[1,16,1,8,8,512]{5,4,3,1,2,0:T(8,128)(2,1)S(1)} reshape(bf16[16,64,16,32]{3,2,1,0:T(8,128)(2,1)} %copy.51) | data formatting | bytes 2097152 | tf_op jit(solution)/shard_map/reshape;reshape | solution.py:97
  275.4 2.8 fusion.42
  278.2 0.6 copy.54
  278.8 31.2 %all_to_all.24 = bf16[1,128,8,1,512]{4,2,3,0,1:T(8,128)(2,1)S(1)} all-to-all(bf16[1,128,8,1,512]{4,2,3,0,1:T(8,128)(2,1)S(1)} %copy.54), channel_id=1, replica_groups=mesh['dp'=16,'space'=16] {'space'}, dimensions={1} | all-to-all | bytes 2097152 | tf_op jit(solution)/shard_map/all_to_all | solution.py:155
  310.1 1.5 copy.55
  (32 shorter events, 2.1 us)
Async XLA Ops:
  6.5 70.5 %copy-start.5 = (f32[2048]{0:T(1024)S(1)}, f32[2048]{0:T(1024)}, u32[]{:S(2)}) copy-start(f32[2048]{0:T(1024)} %param.16) | copy-start | bytes 24580
  6.5 70.5 %all-gather.4.cloned.1.call-start = ((), (), s32[]{:S(2)}) async-start(), calls=%async_computation.2 | async-start | bytes 2228224 | tf_op jit(solution)/shard_map/all_gather | solution.py:38
  7.3 130.9 %all-gather.6.cloned.1.call-start = ((), (), s32[]{:S(2)}) async-start(), calls=%async_computation.3 | async-start | bytes 2228224 | tf_op jit(solution)/shard_map/all_gather | solution.py:65
  9.5 7.4 %collective-permute-start.1 = (bf16[1,1,128,512]{3,2,1,0:T(8,128)(2,1)S(1)}, bf16[1,1,128,512]{3,2,1,0:T(8,128)(2,1)S(1)}, u32[]{:S(2)}, u32[]{:S(2)}) collective-permute-start(bf16[1,1,128,512]{3,2,1,0:T(8,128)(2,1)S(1)} %get-tuple-element.11), channel_id=1, source_target_pairs={{1,0},{2,1},{3,2},{4,3},{5,4},{6,5},{7,6},{8,7},{9,8},{10,9},{11,1... | collective-permute-start | bytes 393224 | tf_op jit(solution)/shard_map/ppermute | solution.py:21
  10.8 6.9 %collective-permute-start = (bf16[1,1,128,512]{3,2,1,0:T(8,128)(2,1)S(1)}, bf16[1,1,128,512]{3,2,1,0:T(8,128)(2,1)S(1)}, u32[]{:S(2)}, u32[]{:S(2)}) collective-permute-start(bf16[1,1,128,512]{3,2,1,0:T(8,128)(2,1)S(1)} %get-tuple-element.10), channel_id=1, source_target_pairs={{0,1},{1,2},{2,3},{3,4},{4,5},{5,6},{6,7},{7,8},{8,9},{9,10},{10,1... | collective-permute-start | bytes 393224 | tf_op jit(solution)/shard_map/ppermute | solution.py:19
  84.0 54.1 %copy-start.1 = (bf16[1,8,128,512]{3,2,1,0:T(8,128)(2,1)S(1)}, bf16[1,8,128,512]{3,2,1,0:T(8,128)(2,1)}, u32[]{:S(2)}) copy-start(bf16[1,8,128,512]{3,2,1,0:T(8,128)(2,1)} %param.12) | copy-start | bytes 3145732
  84.0 54.1 %copy-start.6 = (f32[2048]{0:T(1024)S(1)}, f32[2048]{0:T(1024)}, u32[]{:S(2)}) copy-start(f32[2048]{0:T(1024)} %param.18) | copy-start | bytes 24580
  138.1 34.7 %copy-start.2 = (bf16[512,32]{0,1:T(8,128)(2,1)S(1)}, bf16[512,32]{0,1:T(8,128)(2,1)}, u32[]{:S(2)}) copy-start(bf16[512,32]{0,1:T(8,128)(2,1)} %param.23) | copy-start | bytes 98308
  167.8 51.6 %copy-start.3 = (f32[512]{0:T(512)S(1)}, f32[512]{0:T(512)}, u32[]{:S(2)}) copy-start(f32[512]{0:T(512)} %param.21) | copy-start | bytes 6148
  167.8 51.6 %copy-start.4 = (f32[512]{0:T(512)S(1)}, f32[512]{0:T(512)}, u32[]{:S(2)}) copy-start(f32[512]{0:T(512)} %param.20) | copy-start | bytes 6148
  167.8 50.3 %all-to-all-start = ((bf16[1,8,8,16,512]{4,2,1,0,3:T(8,128)(2,1)}), bf16[1,8,8,16,512]{4,2,1,0,3:T(8,128)(2,1)S(1)}, u32[]{:S(2)}, u32[]{:S(2)}) async-start(bf16[1,8,8,16,512]{4,2,1,0,3:T(8,128)(2,1)} %copy.41), calls=%async_computation | async-start | bytes 2097152 | tf_op jit(solution)/shard_map/all_to_all | solution.py:145
  172.1 63.0 %all-gather.8.cloned.1.call-start = ((), (), s32[]{:S(2)}) async-start(), calls=%async_computation.4 | async-start | bytes 1671168 | tf_op jit(solution)/shard_map/all_gather | solution.py:73
  254.1 6.5 %copy-start = (bf16[16,64,16,32]{3,2,1,0:T(8,128)(2,1)S(1)}, bf16[16,64,16,32]{3,2,1,0:T(8,128)(2,1)}, u32[]{:S(2)}) copy-start(bf16[16,64,16,32]{3,2,1,0:T(8,128)(2,1)} %reshape_reshape.13) | copy-start | bytes 3145732
Sparse Core Ops, SparseCore 0:
  9.9 67.1 all-gather.3
  79.8 58.2 all-gather.5
  175.6 59.3 all-gather.7
where the time goes:
time: 319 us; the launch traced here: 318 us
  waiting for transfers between devices  129 us (40%)
  blocking collectives  76.5 us (24%)
  matrix products  50.6 us (16%)
  local copies, waits for them, and re-layouts  32.4 us (10%)
  between operations  13.3 us (4%)
  starting transfers between devices  10.6 us (3%)
  other arithmetic  5.8 us (2%)
    all_gather x1, waiting for transfers between devices, expand_tokens(): lax.all_gather(w_expand, 'dp', axis=1, tiled=True)  59.1 us
    all_gather x1, waiting for transfers between devices, project_back(): lax.all_gather(w_project, 'dp', axis=1, tiled=True)  51.4 us
    all_gather x1, blocking collectives, out_of(): lax.all_gather(w_out, 'dp', axis=1, tiled=True)  45.3 us
    all_to_all x1, blocking collectives, local(): lax.all_to_all(finished, 'space', split_axis=1, concat_axis=3, tiled=True)  31.2 us
    dot_general x1, matrix products, project_back(): jnp.dot(flat, lax.all_gather(w_project, 'dp', axis=1, tiled=True), prefer...  28.1 us
    all_gather x1, waiting for transfers between devices, qkv_of(): lax.all_gather(w_qkv, 'dp', axis=1, tiled=True)  15.2 us
    dot_general x1, matrix products, expand_tokens(): jnp.dot(flat, lax.all_gather(w_expand, 'dp', axis=1, tiled=True), preferr...  6.92 us
    dot_general x1, matrix products, attend_windows(): jnp.einsum('wqhd,wkhd->whqk', query_heads, key_heads, preferred_element_t...  6.45 us
  transfers between devices with their start and end apart: 6, of which 4 were waited for; matrix products, arithmetic and copies ran while one was open for 4% of the time, Pallas kernels for 0%

commit v1 on v0

v1 whole, which is shorter than its diff:
```python
import jax
import jax.numpy as jnp
from jax import lax
from jax.experimental import pallas as pl
from jax.experimental.pallas import tpu as pltpu
from jax.sharding import PartitionSpec as P

F32 = jnp.float32
BF16 = jnp.bfloat16
NY, NX, NZ = 4, 4, 4
ROWS, COLS, CH, FF = 8, 128, 512, 2048
Q_SCALE = 1.4426950408889634 / (32.0**0.5)


def dot_nn(a, b):
    return jnp.dot(a, b, preferred_element_type=F32)


def dot_nt(a, b):
    return lax.dot_general(a, b, (((1,), (1,)), ((), ())), preferred_element_type=F32)


def gelu(x):
    inner = x * (0.7978845608028654 + 0.035677408136300125 * (x * x))
    half = 0.5 * x
    return half + half * jnp.tanh(inner)


def eye(n):
    return (
        lax.broadcasted_iota(jnp.int32, (n, n), 0) == lax.broadcasted_iota(jnp.int32, (n, n), 1)
    ).astype(BF16)


def kernel(
    f_ref, bns_ref, bnb_ref, wex_ref, be_ref, dwk_ref, dwb_ref, wpr_ref, lng_ref, lnb_ref, wqkv_ref, wout_ref,
    o_ref,
    halo, fperm, xn, we, w1, w2, ebuf, sbuf, co, gbuf, qkv, fin, rbuf,
    wsend, wrecv, hsend, hrecv, asend, arecv, rsend, rrecv,
):
    dp = lax.axis_index("dp")
    sp = lax.axis_index("space")
    core, yy, zh = dp % 2, (dp // 2) % NY, dp // (2 * NY)
    xx, zl = sp // NZ, sp % NZ
    par, half = zl % 2, zl // 2
    mine = 2 * xx + half

    def at(z_hi, y, c, x, z_lo):
        return {"dp": (z_hi * NY + y) * 2 + c, "space": x * NZ + z_lo}

    y_up, y_dn, y_far = (yy + 1) % NY, (yy + NY - 1) % NY, (yy + 2) % NY
    dev_up = at(zh, y_up, core, xx, zl)
    dev_dn = at(zh, y_dn, core, xx, zl)
    dev_sib = at(zh, yy, 1 - core, xx, zl)
    dev_mir = at(1 - zh, yy, core, xx, NZ - 1 - zl)
    dev_next = {"dp": dp, "space": (sp + 1) % 16}
    dev_prev = {"dp": dp, "space": (sp + 15) % 16}

    def member(k):
        return {"dp": dp, "space": (k // 2) * NZ + (k % 2) * 2 + par}

    barrier = pltpu.get_barrier_semaphore()
    peers = [dev_up, dev_dn, dev_sib, dev_mir, dev_next, dev_prev]
    peers += [member((mine + m) % 8) for m in range(1, 8)]
    for peer in peers:
        pl.semaphore_signal(barrier, inc=1, device_id=peer)
    pl.semaphore_wait(barrier, len(peers))

    pending = []

    def remote(src, dst, send, recv, dev):
        return pltpu.make_async_remote_copy(
            src_ref=src, dst_ref=dst, send_sem=send, recv_sem=recv, device_id=dev
        )

    def push(src, dst, send, recv, dev):
        copy = remote(src, dst, send, recv, dev)
        copy.start()
        pending.append(copy)

    def shard(z_hi, y, c):
        return (z_hi * NY + y) * 2 + c

    bufs = (we, w1, w2)
    own_d = shard(zh, yy, core)
    oth = 1 - zh

    def wpush(ph, slot, d, dev, src=None, lo=None, n=None):
        dst = bufs[ph].at[d] if lo is None else bufs[ph].at[d, pl.ds(lo, n)]
        push(dst if src is None else src, dst, wsend.at[ph, slot], wrecv.at[ph, slot], dev)

    def wwait(ph, slot, d, lo=None, n=None):
        dst = bufs[ph].at[d] if lo is None else bufs[ph].at[d, pl.ds(lo, n)]
        remote(dst, dst, wsend.at[ph, slot], wrecv.at[ph, slot], dev_sib).wait_recv()

    halves = tuple(b.shape[1] // 2 for b in bufs)

    def g_start(ph, src=None):
        wpush(ph, 0, own_d, dev_up, src)
        wpush(ph, 1, own_d, dev_dn, src)
        wpush(ph, 2, own_d, dev_mir, src)
        wpush(ph, 3, own_d, dev_sib, src)

    def g_ring(ph, z_hi, base, sib):
        n = halves[ph]
        up_slot, dn_slot = (0, 1) if base == 4 else (8, 9)
        d_dn, d_up = shard(z_hi, y_dn, core), shard(z_hi, y_up, core)
        wwait(ph, up_slot, d_dn)
        wpush(ph, base, d_dn, dev_up, None, 0, n)
        wwait(ph, dn_slot, d_up)
        wpush(ph, base + 1, d_up, dev_dn, None, n, n)
        wpush(ph, sib, d_dn, dev_sib)
        wpush(ph, sib + 1, d_up, dev_sib)

    def g_ev1(ph):
        g_ring(ph, zh, 4, 6)
        d = shard(oth, yy, core)
        wwait(ph, 2, d)
        wpush(ph, 8, d, dev_up)
        wpush(ph, 9, d, dev_dn)
        wpush(ph, 10, d, dev_sib)

    def g_far(ph, z_hi, base, sib):
        n = halves[ph]
        d = shard(z_hi, y_far, core)
        wwait(ph, base, d, 0, n)
        wwait(ph, base + 1, d, n, n)
        wpush(ph, sib, d, dev_sib)

    def g_ev2(ph):
        g_ring(ph, oth, 11, 13)

    def g_ev3(ph):
        g_far(ph, zh, 4, 15)

    def g_ev4(ph):
        g_far(ph, oth, 11, 16)

    def sib_wait(ph, slot, z_hi, y):
        wwait(ph, slot, shard(z_hi, y, 1 - core))

    def sib_all(ph):
        sib_wait(ph, 3, zh, yy)
        sib_wait(ph, 6, zh, y_dn)
        sib_wait(ph, 7, zh, y_up)
        sib_wait(ph, 10, oth, yy)
        sib_wait(ph, 13, oth, y_dn)
        sib_wait(ph, 14, oth, y_up)
        sib_wait(ph, 15, zh, y_far)
        sib_wait(ph, 16, oth, y_far)

    g_start(0, wex_ref)
    push(f_ref.at[ROWS - 1], halo.at[0], hsend.at[0], hrecv.at[0], dev_next)
    push(f_ref.at[0], halo.at[1], hsend.at[1], hrecv.at[1], dev_prev)

    we[own_d] = wex_ref[...]
    w1[own_d] = dot_nt(eye(32), wpr_ref[...]).astype(BF16)
    w2[own_d, 0:96] = dot_nt(eye(96), wqkv_ref[...]).astype(BF16)
    w2[own_d, 96:128] = dot_nt(eye(32), wout_ref[...]).astype(BF16)

    tok = lax.broadcasted_iota(jnp.int32, (COLS, COLS), 0)
    col = lax.broadcasted_iota(jnp.int32, (COLS, COLS), 1)
    perm = ((tok % 8) * 16 + tok // 8 == col).astype(BF16)
    unperm = ((tok % 16) * 8 + tok // 16 == col).astype(BF16)

    def prep(row, value):
        moved = dot_nn(perm, value)
        xn[row] = (moved * bns_ref[...] + bnb_ref[...]).astype(BF16)
        return moved.astype(BF16)

    @pl.loop(0, ROWS)
    def _(r):
        fperm[r] = prep(r + 1, f_ref[r])

    remote(halo.at[0], halo.at[0], hsend.at[0], hrecv.at[0], dev_next).wait_recv()
    remote(halo.at[1], halo.at[1], hsend.at[1], hrecv.at[1], dev_prev).wait_recv()
    prep(0, halo[0])
    prep(ROWS + 1, halo[1])

    sub = lax.broadcasted_iota(jnp.int32, (2, 8, 128), 1)

    def expand(g):
        @pl.loop(0, (ROWS + 2) // 2)
        def _(r2):
            x = xn[pl.ds(2 * r2, 2)].reshape(2 * COLS, CH)
            w = jnp.concatenate([we[2 * g], we[2 * g + 1]], axis=1)
            bias = be_ref[:, pl.ds(pl.multiple_of(256 * g, 256), 256)]
            e = gelu(dot_nn(x, w) + bias)
            for k in range(2):
                part = e[:, 128 * k : 128 * (k + 1)].reshape(2, 16, 8, 128)
                rows = pl.ds(2 * r2, 2)
                ebuf[2 * g + k, rows, 1:17] = part
                before = pltpu.roll(part[:, 15], 1, 1)
                ebuf[2 * g + k, rows, 0] = jnp.where(sub == 0, 0.0, before)
                after = pltpu.roll(part[:, 0], 7, 1)
                ebuf[2 * g + k, rows, 17] = jnp.where(sub == 7, 0.0, after)

    def pair(z_hi, y):
        return z_hi * NY + y

    sib_wait(0, 3, zh, yy)
    expand(pair(zh, yy))
    g_ev1(0)
    sib_wait(0, 6, zh, y_dn)
    expand(pair(zh, y_dn))
    sib_wait(0, 7, zh, y_up)
    expand(pair(zh, y_up))
    g_ev2(0)
    g_start(1)
    g_ev3(0)
    sib_wait(0, 10, oth, yy)
    expand(pair(oth, yy))
    g_ev4(0)
    sib_wait(0, 15, zh, y_far)
    expand(pair(zh, y_far))
    g_ev1(1)
    sib_wait(0, 13, oth, y_dn)
    expand(pair(oth, y_dn))
    sib_wait(0, 14, oth, y_up)
    expand(pair(oth, y_up))
    g_ev2(1)
    sib_wait(0, 16, oth, y_far)
    expand(pair(oth, y_far))
    g_start(2)
    g_ev3(1)

    @pl.when(sp == 0)
    def _():
        ebuf[:, 0] = jnp.zeros((16, 18, 8, 128), F32)

    @pl.when(sp == 15)
    def _():
        ebuf[:, ROWS + 1] = jnp.zeros((16, 18, 8, 128), F32)

    def conv(q):
        @pl.loop(0, 8)
        def _(g):
            for k in range(2):
                lanes = pl.ds(pl.multiple_of(256 * g + 128 * k, 128), 128)
                taps = dwk_ref[:, lanes]
                bias = dwb_ref[:, lanes]
                for r in range(2):
                    acc = jnp.broadcast_to(bias[None], (16, 8, 128))
                    for i in range(3):
                        for j in range(3):
                            t = 3 * i + j
                            acc = acc + ebuf[2 * g + k, 2 * q + r + i, j : j + 16] * taps[t : t + 1][None]
                    sbuf[g, 128 * r : 128 * (r + 1), 128 * k : 128 * (k + 1)] = (
                        gelu(acc).astype(BF16).reshape(128, 128)
                    )

    def project(q):
        w = w1[...].reshape(CH, FF)
        total = fperm[pl.ds(2 * q, 2)].reshape(2 * COLS, CH).astype(F32)
        for g in range(8):
            total = total + dot_nt(sbuf[g], w[:, 256 * g : 256 * (g + 1)])
        co[pl.ds(2 * q, 2)] = total.astype(BF16).reshape(2, COLS, CH)

    def forward(t, q, u):
        e = half if u == 0 else 1 - half
        push(
            co.at[2 * q + e], gbuf.at[mine], asend.at[2 * t + u], arecv.at[2 * t + u], member(2 * q + e)
        )

    def arrived(t, u):
        e = half if u == 0 else 1 - half
        src = 2 * ((xx + 3 - t) % NX) + e
        remote(
            gbuf.at[src], gbuf.at[src], asend.at[2 * t + u], arecv.at[2 * t + u], member(src)
        ).wait_recv()

    for t in range(4):
        q = (xx + 1 + t) % NX
        conv(q)
        if t == 0:
            g_ev4(1)
            sib_all(1)
        project(q)
        if t < 3:
            forward(t, q, 1)
            forward(t, q, 0)
        else:
            forward(t, q, 1)
            gbuf[mine] = co[mine]
        if t == 0:
            g_ev1(2)
        if t == 1:
            g_ev2(2)
            g_ev3(2)
        if t == 2:
            g_ev4(2)
    sib_all(2)

    def tokens_of(i2):
        values = gbuf[pl.ds(2 * i2, 2)].reshape(2 * COLS, CH).astype(F32)
        center = jnp.mean(values, axis=-1, keepdims=True)
        off = values - center
        spread = jnp.mean(off * off, axis=-1, keepdims=True)
        ln = (off * lax.rsqrt(spread + 1e-05) * lng_ref[...] + lnb_ref[...]).astype(BF16)
        w = w2[:, 0:96].reshape(3 * CH, CH)
        rows = pl.ds(2 * i2, 2)
        qkv[rows, :, 0:CH] = (dot_nt(ln, w[0:CH]) * Q_SCALE).astype(BF16).reshape(2, COLS, CH)
        qkv[rows, :, CH : 2 * CH] = dot_nt(ln, w[CH : 2 * CH]).astype(BF16).reshape(2, COLS, CH)
        qkv[rows, :, 2 * CH :] = dot_nt(ln, w[2 * CH :]).astype(BF16).reshape(2, COLS, CH)

    for t in range(4):
        if t < 3:
            arrived(t, 0)
        arrived(t, 1)
        tokens_of((xx + 3 - t) % NX)

    lane = lax.broadcasted_iota(jnp.int32, (128, 128), 1)
    row = lax.broadcasted_iota(jnp.int32, (128, 128), 0)
    heads = [(lane // 32 == n) for n in range(4)]
    same = (lane // 8) % 2 == (row // 8) % 2
    same4 = jnp.concatenate([same] * 4, axis=0)

    def windows(bp):
        rows = pl.ds(pl.multiple_of(16 * bp, 16), 16)
        parts = []
        for gr in range(4):
            lo = 128 * gr
            qv = qkv[:, rows, lo : lo + 128].reshape(128, 128)
            kv = qkv[:, rows, CH + lo : CH + lo + 128].reshape(128, 128)
            vv = qkv[:, rows, 2 * CH + lo : 2 * CH + lo + 128].reshape(128, 128)
            zero = jnp.zeros_like(qv)
            qm = jnp.concatenate([jnp.where(m, qv, zero) for m in heads], axis=0)
            vm = jnp.concatenate([jnp.where(m, vv, zero) for m in heads], axis=0)
            e = jnp.where(same4, jnp.exp2(dot_nt(qm, kv)), 0.0)
            p = (e * (1.0 / jnp.sum(e, axis=1, keepdims=True))).astype(BF16)
            wide = jnp.concatenate([p[128 * n : 128 * (n + 1)] for n in range(4)], axis=1)
            parts.append(dot_nn(wide, vm).astype(BF16))
        return jnp.concatenate(parts, axis=1)

    for c in range(4):
        @pl.loop(2 * c, 2 * c + 2)
        def _(bp):
            rows = pl.ds(pl.multiple_of(16 * bp, 16), 16)
            wo = w2[:, 96:128].reshape(CH, CH)
            done = dot_nt(windows(bp), wo) + gbuf[:, rows].reshape(128, CH).astype(F32)
            fin[:, rows] = done.astype(BF16).reshape(8, 16, CH)

        span = pl.ds(32 * c, 32)
        for m in range(1, 8):
            k = (mine + m) % 8
            push(
                fin.at[k, span], rbuf.at[mine, span], rsend.at[c, m - 1], rrecv.at[c, m - 1], member(k)
            )

    o_ref[mine] = dot_nn(unperm, fin[mine]).astype(BF16)
    for m in range(1, 8):
        k = (mine + 8 - m) % 8
        for c in range(4):
            span = pl.ds(32 * c, 32)
            remote(
                rbuf.at[k, span], rbuf.at[k, span], rsend.at[c, m - 1], rrecv.at[c, m - 1], member(k)
            ).wait_recv()
        o_ref[k] = dot_nn(unperm, rbuf[k]).astype(BF16)

    for copy in pending:
        copy.wait_send()


def local(
    fields, bn_scale, bn_shift, w_expand, expand_bias, dw_kernel, dw_bias, w_project, ln_gain, ln_bias, w_qkv, w_out
):
    vmem = pl.BlockSpec(memory_space=pltpu.VMEM)
    dma = pltpu.SemaphoreType.DMA
    out = pl.pallas_call(
        kernel,
        out_shape=jax.ShapeDtypeStruct((ROWS, COLS, CH), BF16),
        in_specs=[vmem] * 12,
        out_specs=vmem,
        scratch_shapes=[
            pltpu.VMEM((2, COLS, CH), BF16),
            pltpu.VMEM((ROWS, COLS, CH), BF16),
            pltpu.VMEM((ROWS + 2, COLS, CH), BF16),
            pltpu.VMEM((16, CH, 128), BF16),
            pltpu.VMEM((16, 32, FF), BF16),
            pltpu.VMEM((16, 128, CH), BF16),
            pltpu.VMEM((16, ROWS + 2, 18, 8, 128), F32),
            pltpu.VMEM((8, 256, 256), BF16),
            pltpu.VMEM((ROWS, COLS, CH), BF16),
            pltpu.VMEM((ROWS, COLS, CH), BF16),
            pltpu.VMEM((ROWS, COLS, 3 * CH), BF16),
            pltpu.VMEM((ROWS, COLS, CH), BF16),
            pltpu.VMEM((ROWS, COLS, CH), BF16),
            dma((3, 17)),
            dma((3, 17)),
            dma((2,)),
            dma((2,)),
            dma((8,)),
            dma((8,)),
            dma((4, 7)),
            dma((4, 7)),
        ],
        compiler_params=pltpu.CompilerParams(
            collective_id=0, has_side_effects=True, vmem_limit_bytes=60 * 1024 * 1024
        ),
    )(
        fields.reshape(ROWS, COLS, CH),
        bn_scale.reshape(1, CH),
        bn_shift.reshape(1, CH),
        w_expand,
        expand_bias.reshape(1, FF),
        dw_kernel.reshape(9, FF),
        dw_bias.reshape(1, FF),
        w_project,
        ln_gain.reshape(1, CH),
        ln_bias.reshape(1, CH),
        w_qkv,
        w_out,
    )
    return out.reshape(fields.shape)


def solution(mesh):
    in_specs = (
        P("dp", "space", None, None),
        P(),
        P(),
        P(None, "dp"),
        P(),
        P(),
        P(),
        P(None, "dp"),
        P(),
        P(),
        P(None, "dp"),
        P(None, "dp"),
    )
    out_specs = P("dp", "space", None, None)
    return jax.shard_map(local, mesh=mesh, in_specs=in_specs, out_specs=out_specs, check_vma=False)
```

time: 319 us -> 102 us (0.32)
  waiting for transfers between devices: 129 us -> 0 us
  Pallas kernels: 0 us -> 95.5 us
  blocking collectives: 76.5 us -> 0 us
  matrix products: 50.6 us -> 0 us
  local copies, waits for them, and re-layouts: 32.4 us -> 6.55 us
  between operations: 13.3 us -> 0.01 us
  starting transfers between devices: 10.6 us -> 0 us
  other arithmetic: 5.8 us -> 0 us
    all_gather x3 -> x0, waiting for transfers between devices: 126 us -> none  [the longest x1 59.1 us: expand_tokens(): lax.all_gather(w_expand, 'dp', axis=1, tiled=True)]
    pallas_call x0 -> x1, Pallas kernels: none -> 95.5 us  [local(): pl.pallas_call(kernel, out_shape=jax.ShapeDtypeStruct((ROWS, COLS, CH), B...]
    dot_general x6 -> x0, matrix products: 50.6 us -> none  [the longest x1 28.1 us: project_back(): jnp.dot(flat, lax.all_gather(w_project, 'dp', axis=1, tiled=True), prefer...]
    all_gather x1 -> x0, blocking collectives: 45.3 us -> none  [out_of(): lax.all_gather(w_out, 'dp', axis=1, tiled=True)]
    all_to_all x1 -> x0, blocking collectives: 31.2 us -> none  [local(): lax.all_to_all(finished, 'space', split_axis=1, concat_axis=3, tiled=True)]
    another operation x4 -> x0, local copies, waits for them, and re-layouts: 17.4 us -> none  [the longest x1 5.93 us: from_windows(): split = windows.reshape(items, stride_rows, blocks_here, GRID, GRID, width)]
    ppermute x2 -> x0, starting transfers between devices: 6.29 us -> none  [the longest x1 5 us: padded_2(): lax.ppermute(tail, axis, [(i, (i + 1) % count) for i in range(ends)])]
    convert_element_type x2 -> x0, local copies, waits for them, and re-layouts: 6.28 us -> none  [the longest x1 5.7 us: attend_windows(): return mixed.astype(jnp.bfloat16).reshape(window_count, length, width)]
  transfers between devices with their start and end apart: 6 -> 0, of which waited for: 4 -> 0; matrix products, arithmetic and copies ran while one was open for 4% -> 0% of each run, Pallas kernels for 0% -> 0%
where the time goes in v1:
time: 102 us
  Pallas kernels  95.5 us (94%)
  local copies, waits for them, and re-layouts  6.55 us (6%)
    pallas_call x1, Pallas kernels, local(): pl.pallas_call(kernel, out_shape=jax.ShapeDtypeStruct((ROWS, COLS, CH), B...  95.5 us
    unnamed x10, local copies, waits for them, and re-layouts  4.94 us

profile of v1, /device:TPU:1, one launch (start us, length us, event | category | flops | bytes accessed | tf_op | source)
XLA Modules:
  0.0 102.0 jit_solution(6469288769832074238)
XLA Ops:
  0.0 0.0 copy-start.1
  0.0 1.6 %reshape.31.dwk_ref = f32[9,2048]{1,0:T(8,128)} reshape(f32[3,3,2048]{2,1,0:T(4,128)} %param.17) | data formatting | bytes 147456 | tf_op jit(solution)/shard_map/reshape | solution.py:406
  1.6 0.0 copy-done.1
  1.6 0.0 copy-start.2
  1.6 0.8 copy.14.wqkv_ref
  2.4 0.0 copy-done.2
  2.4 0.0 copy-start
  2.4 0.8 copy.15.wout_ref
  3.2 0.1 copy-done
  3.3 1.0 copy.13.wpr_ref
  4.3 95.5 %shard_map.118 = bf16[8,128,512]{2,1,0:T(8,128)(2,1)} custom-call(bf16[8,128,512]{2,1,0:T(8,128)(2,1)} %bitcast.9, f32[1,512]{1,0:T(1,128)} %bitcast.12, f32[1,512]{1,0:T(1,128)} %bitcast.13, bf16[512,128]{1,0:T(8,128)(2,1)} %wex_ref.1, f32[1,2048]{1,0:T(1,128)} %bitcast.10, f32[9,2048]{1,0:T(8,128)} %reshape.31.dwk_ref, f32[1,2048]{1,0:T(1,128)} %bitcast.11, ...), custom_call_target="tpu_custom_call" | custom-call | tf_op jit(solution)/shard_map/pallas_call | solution.py:369
  99.8 2.3 %copy.17 = bf16[1,8,128,512]{3,2,1,0:T(8,128)(2,1)} copy(bf16[1,8,128,512]{3,2,1,0:T(8,128)(2,1)} %bitcast.8) | data formatting | bytes 2097152
Async XLA Ops:
  0.0 1.6 %copy-start.1 = (bf16[512,96]{0,1:T(8,128)(2,1)S(1)}, bf16[512,96]{0,1:T(8,128)(2,1)}, u32[]{:S(2)}) copy-start(bf16[512,96]{0,1:T(8,128)(2,1)} %param.22) | copy-start | bytes 294916
  1.6 0.8 copy-start.2
  2.4 0.9 copy-start

commit v2 on v1

v2 whole, which is shorter than its diff:
```python
import jax
import jax.numpy as jnp
from jax import lax
from jax.experimental import pallas as pl
from jax.experimental.pallas import tpu as pltpu
from jax.sharding import PartitionSpec as P

F32 = jnp.float32
BF16 = jnp.bfloat16
NY, NX, NZ = 4, 4, 4
ROWS, COLS, CH, FF = 8, 128, 512, 2048
Q_SCALE = 1.4426950408889634 / (32.0**0.5)


def dot_nn(a, b):
    return jnp.dot(a, b, preferred_element_type=F32)


def dot_nt(a, b):
    return lax.dot_general(a, b, (((1,), (1,)), ((), ())), preferred_element_type=F32)


def gelu(x):
    inner = x * (0.7978845608028654 + 0.035677408136300125 * (x * x))
    half = 0.5 * x
    return half + half * jnp.tanh(inner)


def kernel(
    f_ref, bns_ref, bnb_ref, wex_ref, be_ref, dwk_ref, dwb_ref, wpr_ref, lng_ref, lnb_ref, wqkv_ref, wout_ref,
    o_ref,
    fbuf, halo, fperm, xn, we, w1, w2, ebuf, sbuf, co, gbuf, qkv, fin,
    lsem, wsend, wrecv, hsend, hrecv, asend, arecv, rsend, rrecv,
):
    dp = lax.axis_index("dp")
    sp = lax.axis_index("space")
    core, yy, zh = dp % 2, (dp // 2) % NY, dp // (2 * NY)
    xx, zl = sp // NZ, sp % NZ
    par, half = zl % 2, zl // 2
    mine = 2 * xx + half

    def at(z_hi, y, c, x, z_lo):
        return {"dp": (z_hi * NY + y) * 2 + c, "space": x * NZ + z_lo}

    y_up, y_dn, y_far = (yy + 1) % NY, (yy + NY - 1) % NY, (yy + 2) % NY
    dev_up = at(zh, y_up, core, xx, zl)
    dev_dn = at(zh, y_dn, core, xx, zl)
    dev_far = at(zh, y_far, core, xx, zl)
    dev_sib = at(zh, yy, 1 - core, xx, zl)
    dev_mir = at(1 - zh, yy, core, xx, NZ - 1 - zl)
    dev_xup = at(zh, yy, core, (xx + 1) % NX, zl)
    dev_xdn = at(zh, yy, core, (xx + NX - 1) % NX, zl)
    dev_next = {"dp": dp, "space": (sp + 1) % 16}
    dev_prev = {"dp": dp, "space": (sp + 15) % 16}

    def member(k):
        return {"dp": dp, "space": (k // 2) * NZ + (k % 2) * 2 + par}

    barrier = pltpu.get_barrier_semaphore()
    peers = [dev_up, dev_dn, dev_far, dev_sib, dev_mir, dev_next, dev_prev]
    peers += [member((mine + m) % 8) for m in range(1, 8)]
    for peer in peers:
        pl.semaphore_signal(barrier, inc=1, device_id=peer)

    pending = []

    def remote(src, dst, send, recv, dev):
        return pltpu.make_async_remote_copy(
            src_ref=src, dst_ref=dst, send_sem=send, recv_sem=recv, device_id=dev
        )

    def push(src, dst, send, recv, dev):
        copy = remote(src, dst, send, recv, dev)
        copy.start()
        pending.append(copy)

    def shard(z_hi, y, c):
        return (z_hi * NY + y) * 2 + c

    own_d = shard(zh, yy, core)
    oth = 1 - zh
    bufs = (we, w1, w2)

    loads = [
        pltpu.make_async_copy(wex_ref, we.at[own_d], lsem.at[0]),
        pltpu.make_async_copy(wpr_ref, w1.at[own_d], lsem.at[1]),
        pltpu.make_async_copy(f_ref, fbuf, lsem.at[2]),
        pltpu.make_async_copy(wqkv_ref, w2.at[own_d, 0:96], lsem.at[3]),
        pltpu.make_async_copy(wout_ref, w2.at[own_d, 96:128], lsem.at[4]),
    ]
    for load in loads:
        load.start()
    pl.semaphore_wait(barrier, len(peers))

    odd = xx % 2
    unit = (128, 512, 32)

    def piece(ph, d, first, count):
        span = pl.ds(pl.multiple_of(first * unit[ph], unit[ph]), count * unit[ph])
        return bufs[ph].at[d, :, span] if ph == 1 else bufs[ph].at[d, span]

    places = [
        (oth, yy), (zh, y_dn), (zh, y_up), (zh, y_far), (oth, y_dn), (oth, y_up), (oth, y_far), (zh, yy)
    ]

    def wpush(ph, slot, ref, dev):
        push(ref, ref, wsend.at[ph, slot], wrecv.at[ph, slot], dev)

    def wwait(ph, slot, ref):
        remote(ref, ref, wsend.at[ph, slot], wrecv.at[ph, slot], dev_sib).wait_recv()

    def carried(ph, i):
        return piece(ph, shard(*places[i], core), 2 * odd, 2)

    def spread(ph, i, base):
        ref = carried(ph, i)
        wpush(ph, base, ref, dev_up)
        wpush(ph, base + 1, ref, dev_dn)
        wpush(ph, base + 2, ref, dev_far)

    def g_start(ph):
        wpush(ph, 0, carried(ph, 7), dev_mir)
        spread(ph, 7, 1)
        wpush(ph, 21, bufs[ph].at[own_d], dev_sib)

    def g_arrive(ph, *which):
        for i in which:
            wwait(ph, i, carried(ph, i))
            if i == 0:
                spread(ph, 0, 4)
            d = shard(*places[i], core)
            wpush(ph, 7 + 2 * i, piece(ph, d, 2 * odd, 1), dev_xup)
            wpush(ph, 8 + 2 * i, piece(ph, d, 2 * odd + 1, 1), dev_xdn)

    def g_finish(ph, *which):
        for i in which:
            d = shard(*places[i], core)
            wwait(ph, 7 + 2 * i, piece(ph, d, 2 - 2 * odd, 1))
            wwait(ph, 8 + 2 * i, piece(ph, d, 3 - 2 * odd, 1))
            wpush(ph, 22 + i, bufs[ph].at[d], dev_sib)

    def sib_wait(ph, *which):
        for i in which:
            slot = 21 if i == 7 else 22 + i
            wwait(ph, slot, bufs[ph].at[shard(*places[i], 1 - core)])

    loads[0].wait()
    g_start(0)
    push(f_ref.at[ROWS - 1], halo.at[0], hsend.at[0], hrecv.at[0], dev_next)
    push(f_ref.at[0], halo.at[1], hsend.at[1], hrecv.at[1], dev_prev)
    loads[1].wait()
    g_start(1)

    tok = lax.broadcasted_iota(jnp.int32, (COLS, COLS), 0)
    col = lax.broadcasted_iota(jnp.int32, (COLS, COLS), 1)
    perm = ((tok % 8) * 16 + tok // 8 == col).astype(BF16)

    def prep(row, value):
        moved = dot_nn(perm, value)
        xn[row] = (moved * bns_ref[...] + bnb_ref[...]).astype(BF16)
        return moved.astype(BF16)

    loads[2].wait()

    @pl.loop(0, ROWS)
    def _(r):
        fperm[r] = prep(r + 1, fbuf[r])

    sub = lax.broadcasted_iota(jnp.int32, (2, 8, 128), 1)

    def expanded(x, g):
        w = jnp.concatenate([we[2 * g], we[2 * g + 1]], axis=1)
        bias = be_ref[:, pl.ds(pl.multiple_of(256 * g, 256), 256)]
        return gelu(dot_nn(x, w) + bias)

    def store(g, e, put):
        for k in range(2):
            part = e[:, 128 * k : 128 * (k + 1)].reshape(2, 16, 8, 128)
            before = jnp.where(sub == 0, 0.0, pltpu.roll(part[:, 15], 1, 1))
            after = jnp.where(sub == 7, 0.0, pltpu.roll(part[:, 0], 7, 1))
            put(2 * g + k, slice(1, 17), part)
            put(2 * g + k, 0, before)
            put(2 * g + k, 17, after)

    def expand(i):
        z_hi, y = places[i]
        g = z_hi * NY + y

        @pl.loop(0, ROWS // 2)
        def _(r2):
            rows = pl.ds(2 * r2 + 1, 2)

            def put(l, b, value):
                ebuf[l, rows, b] = value

            store(g, expanded(xn[rows].reshape(2 * COLS, CH), g), put)

    def expand_rim():
        remote(halo.at[0], halo.at[0], hsend.at[0], hrecv.at[0], dev_next).wait_recv()
        remote(halo.at[1], halo.at[1], hsend.at[1], hrecv.at[1], dev_prev).wait_recv()
        prep(0, halo[0])
        prep(ROWS + 1, halo[1])

        @pl.loop(0, 8)
        def _(g):
            x = jnp.concatenate([xn[0], xn[ROWS + 1]], axis=0)

            def put(l, b, value):
                ebuf[l, 0, b] = value[0]
                ebuf[l, ROWS + 1, b] = value[1]

            store(g, expanded(x, g), put)

        @pl.when(sp == 0)
        def _():
            ebuf[:, 0] = jnp.zeros((16, 18, 8, 128), F32)

        @pl.when(sp == 15)
        def _():
            ebuf[:, ROWS + 1] = jnp.zeros((16, 18, 8, 128), F32)

    sib_wait(0, 7)
    g_arrive(0, 1, 2, 3)
    expand(7)
    g_arrive(0, 0)
    g_finish(0, 1, 2, 3)
    sib_wait(0, 1)
    expand(1)
    g_arrive(1, 1, 2, 3)
    g_finish(0, 0)
    sib_wait(0, 2)
    expand(2)
    g_arrive(1, 0)
    sib_wait(0, 3)
    expand(3)
    g_arrive(0, 4, 5, 6)
    sib_wait(0, 0)
    expand(0)
    g_finish(0, 4, 5, 6)
    loads[3].wait()
    loads[4].wait()
    g_start(2)
    g_finish(1, 1, 2, 3, 0)
    sib_wait(0, 4)
    expand(4)
    g_arrive(1, 4, 5, 6)
    sib_wait(0, 5)
    expand(5)
    sib_wait(0, 6)
    expand(6)
    g_finish(1, 4, 5, 6)
    expand_rim()

    def conv(q):
        @pl.loop(0, 8)
        def _(g):
            for k in range(2):
                lanes = pl.ds(pl.multiple_of(256 * g + 128 * k, 128), 128)
                bias = dwb_ref[:, lanes]
                for r in range(2):
                    acc = jnp.broadcast_to(bias[None], (16, 8, 128))
                    for i in range(3):
                        for j in range(3):
                            tap = dwk_ref[i, j : j + 1, lanes]
                            acc = acc + ebuf[2 * g + k, 2 * q + r + i, j : j + 16] * tap[None]
                    sbuf[g, 128 * r : 128 * (r + 1), 128 * k : 128 * (k + 1)] = (
                        gelu(acc).astype(BF16).reshape(128, 128)
                    )

    def project(q):
        w = w1[...].reshape(CH, FF)
        total = fperm[2 * q : 2 * q + 2].reshape(2 * COLS, CH).astype(F32)
        for g in range(8):
            total = total + dot_nt(sbuf[g], w[:, 256 * g : 256 * (g + 1)])
        co[2 * q : 2 * q + 2] = total.astype(BF16).reshape(2, COLS, CH)

    def group(k):
        return pl.ds(pl.multiple_of(16 * k, 16), 16)

    def forward(q):
        rows = pl.ds(2 * q, 2)
        for m in range(1, 8):
            k = (mine + m) % 8
            push(
                co.at[rows, group(k)], gbuf.at[rows, mine], asend.at[q, m - 1], arecv.at[q, m - 1], member(k)
            )
        gbuf[rows, mine] = co[rows, group(mine)]

    def arrived(q):
        rows = pl.ds(2 * q, 2)
        for m in range(1, 8):
            k = (mine + 8 - m) % 8
            ref = gbuf.at[rows, k]
            remote(ref, ref, asend.at[q, m - 1], arecv.at[q, m - 1], member(k)).wait_recv()

    lane = lax.broadcasted_iota(jnp.int32, (128, 128), 1)
    row = lax.broadcasted_iota(jnp.int32, (128, 128), 0)
    heads = [(lane // 32 == n) for n in range(4)]
    same = (lane // 8) % 2 == (row // 8) % 2
    same4 = jnp.concatenate([same] * 4, axis=0)

    def attend(q):
        held = gbuf[2 * q : 2 * q + 2].reshape(256, CH).astype(F32)
        center = jnp.mean(held, axis=-1, keepdims=True)
        off = held - center
        spread_of = jnp.mean(off * off, axis=-1, keepdims=True)
        ln = (off * lax.rsqrt(spread_of + 1e-05) * lng_ref[...] + lnb_ref[...]).astype(BF16)
        w = w2[:, 0:96].reshape(3 * CH, CH)
        qkv[:, 0:CH] = (dot_nt(ln, w[0:CH]) * Q_SCALE).astype(BF16)
        qkv[:, CH : 2 * CH] = dot_nt(ln, w[CH : 2 * CH]).astype(BF16)
        qkv[:, 2 * CH :] = dot_nt(ln, w[2 * CH :]).astype(BF16)

        @pl.loop(0, 2)
        def _(r):
            rows = pl.ds(pl.multiple_of(128 * r, 128), 128)
            parts = []
            for gr in range(4):
                lo = 128 * gr
                qv = qkv[rows, lo : lo + 128]
                kv = qkv[rows, CH + lo : CH + lo + 128]
                vv = qkv[rows, 2 * CH + lo : 2 * CH + lo + 128]
                zero = jnp.zeros_like(qv)
                qm = jnp.concatenate([jnp.where(m, qv, zero) for m in heads], axis=0)
                vm = jnp.concatenate([jnp.where(m, vv, zero) for m in heads], axis=0)
                e = jnp.where(same4, jnp.exp2(dot_nt(qm, kv)), 0.0)
                p = (e * (1.0 / jnp.sum(e, axis=1, keepdims=True))).astype(BF16)
                wide = jnp.concatenate([p[128 * n : 128 * (n + 1)] for n in range(4)], axis=1)
                parts.append(dot_nn(wide, vm).astype(BF16))
            done = dot_nt(jnp.concatenate(parts, axis=1), w2[:, 96:128].reshape(CH, CH))
            done = done + gbuf[2 * q + r].reshape(128, CH).astype(F32)
            fin[2 * q + r] = done.astype(BF16).reshape(8, 16, CH)

    keeps = []

    def send_back(q):
        rows = pl.ds(2 * q, 2)
        for m in range(1, 8):
            k = (mine + m) % 8
            push(
                fin.at[rows, k], o_ref.at[rows, group(mine)], rsend.at[q, m - 1], rrecv.at[q, m - 1], member(k)
            )
        keep = pltpu.make_async_copy(fin.at[rows, mine], o_ref.at[rows, group(mine)], lsem.at[5 + q])
        keep.start()
        keeps.append(keep)

    def returned(q):
        rows = pl.ds(2 * q, 2)
        for m in range(1, 8):
            k = (mine + 8 - m) % 8
            ref = o_ref.at[rows, group(k)]
            remote(ref, ref, rsend.at[q, m - 1], rrecv.at[q, m - 1], member(k)).wait_recv()

    conv(0)
    sib_wait(1, *range(8))
    project(0)
    forward(0)
    g_arrive(2, 1, 2, 3, 0)
    conv(1)
    project(1)
    forward(1)
    g_arrive(2, 4, 5, 6)
    g_finish(2, 1, 2, 3, 0)
    conv(2)
    project(2)
    forward(2)
    g_finish(2, 4, 5, 6)
    sib_wait(2, *range(8))
    arrived(0)
    attend(0)
    send_back(0)
    conv(3)
    project(3)
    forward(3)
    for q in range(1, 4):
        arrived(q)
        attend(q)
        send_back(q)
    for q in range(4):
        keeps[q].wait()
        returned(q)
    for copy in pending:
        copy.wait_send()


def local(
    fields, bn_scale, bn_shift, w_expand, expand_bias, dw_kernel, dw_bias, w_project, ln_gain, ln_bias, w_qkv, w_out
):
    vmem = pl.BlockSpec(memory_space=pltpu.VMEM)
    hbm = pl.BlockSpec(memory_space=pl.ANY)
    dma = pltpu.SemaphoreType.DMA
    out = pl.pallas_call(
        kernel,
        out_shape=jax.ShapeDtypeStruct((ROWS, COLS, CH), BF16),
        in_specs=[hbm, vmem, vmem, hbm, vmem, vmem, vmem, hbm, vmem, vmem, hbm, hbm],
        out_specs=hbm,
        scratch_shapes=[
            pltpu.VMEM((ROWS, COLS, CH), BF16),
            pltpu.VMEM((2, COLS, CH), BF16),
            pltpu.VMEM((ROWS, COLS, CH), BF16),
            pltpu.VMEM((ROWS + 2, COLS, CH), BF16),
            pltpu.VMEM((16, CH, 128), BF16),
            pltpu.VMEM((16, 32, FF), BF16),
            pltpu.VMEM((16, 128, CH), BF16),
            pltpu.VMEM((16, ROWS + 2, 18, 8, 128), F32),
            pltpu.VMEM((8, 256, 256), BF16),
            pltpu.VMEM((ROWS, COLS, CH), BF16),
            pltpu.VMEM((ROWS, 8, 16, CH), BF16),
            pltpu.VMEM((256, 3 * CH), BF16),
            pltpu.VMEM((ROWS, 8, 16, CH), BF16),
            dma((9,)),
            dma((3, 29)),
            dma((3, 29)),
            dma((2,)),
            dma((2,)),
            dma((4, 7)),
            dma((4, 7)),
            dma((4, 7)),
            dma((4, 7)),
        ],
        compiler_params=pltpu.CompilerParams(
            collective_id=0, has_side_effects=True, vmem_limit_bytes=60 * 1024 * 1024
        ),
    )(
        fields.reshape(ROWS, COLS, CH),
        bn_scale.reshape(1, CH),
        bn_shift.reshape(1, CH),
        w_expand,
        expand_bias.reshape(1, FF),
        dw_kernel,
        dw_bias.reshape(1, FF),
        w_project.T,
        ln_gain.reshape(1, CH),
        ln_bias.reshape(1, CH),
        w_qkv.T,
        w_out.T,
    )
    return out.reshape(ROWS, 16, 8, CH).transpose(0, 2, 1, 3).reshape(fields.shape)


def solution(mesh):
    in_specs = (
        P("dp", "space", None, None),
        P(),
        P(),
        P(None, "dp"),
        P(),
        P(),
        P(),
        P(None, "dp"),
        P(),
        P(),
        P(None, "dp"),
        P(None, "dp"),
    )
    out_specs = P("dp", "space", None, None)
    return jax.shard_map(local, mesh=mesh, in_specs=in_specs, out_specs=out_specs, check_vma=False)
```

time: 102 us -> 93.2 us (0.914)
  Pallas kernels: 95.5 us -> 90.5 us
  local copies, waits for them, and re-layouts: 6.55 us -> 2.55 us
    pallas_call x1, Pallas kernels: 95.5 us -> 90.5 us  [local(): pl.pallas_call(kernel, out_shape=jax.ShapeDtypeStruct((ROWS, COLS, CH), B...]
    unnamed x10 -> x0, local copies, waits for them, and re-layouts: 4.94 us -> none
    transpose x0 -> x1, local copies, waits for them, and re-layouts: none -> 2.55 us  [local(): out.reshape(ROWS, 16, 8, CH).transpose(0, 2, 1, 3).reshape(fields.shape)]
    reshape x1 -> x0, local copies, waits for them, and re-layouts: 1.61 us -> none  [local(): dw_kernel.reshape(9, FF)]
where the time goes in v2:
time: 93.2 us; the launch traced here: 93 us
  Pallas kernels  90.5 us (97%)
  local copies, waits for them, and re-layouts  2.55 us (3%)
    pallas_call x1, Pallas kernels, local(): pl.pallas_call(kernel, out_shape=jax.ShapeDtypeStruct((ROWS, COLS, CH), B...  90.5 us
    transpose x1, local copies, waits for them, and re-layouts, local(): out.reshape(ROWS, 16, 8, CH).transpose(0, 2, 1, 3).reshape(fields.shape)  2.55 us

profile of v2, /device:TPU:1, one launch (start us, length us, event | category | flops | bytes accessed | tf_op | source)
XLA Modules:
  0.0 93.0 jit_solution(3920318711366586989)
XLA Ops:
  0.0 90.5 %shard_map.118 = bf16[8,128,512]{2,1,0:T(8,128)(2,1)} custom-call(bf16[8,128,512]{2,1,0:T(8,128)(2,1)} %bitcast.15, f32[1,512]{1,0:T(1,128)} %bitcast.21, f32[1,512]{1,0:T(1,128)} %bitcast.22, bf16[512,128]{1,0:T(8,128)(2,1)} %wex_ref.1, f32[1,2048]{1,0:T(1,128)} %bitcast.19, f32[3,3,2048]{2,1,0:T(4,128)} %dwk_ref.1, f32[1,2048]{1,0:T(1,128)} %bitcast.20, ...), custom_call_target="tpu_custom_call" | custom-call | tf_op jit(solution)/shard_map/pallas_call | solution.py:391
  90.5 2.5 %copy.13 = bf16[8,8,16,512]{3,2,1,0:T(8,128)(2,1)} copy(bf16[8,8,16,512]{3,1,2,0:T(8,128)(2,1)} %bitcast.14) | data formatting | bytes 2097152 | tf_op jit(solution)/shard_map/transpose | solution.py:437

commit v3 on v2

--- a/solution.py
+++ b/solution.py
@@ -30,14 +30,16 @@
     f_ref, bns_ref, bnb_ref, wex_ref, be_ref, dwk_ref, dwb_ref, wpr_ref, lng_ref, lnb_ref, wqkv_ref, wout_ref,
     o_ref,
     fbuf, halo, fperm, xn, we, w1, w2, ebuf, sbuf, co, gbuf, qkv, fin,
-    lsem, wsend, wrecv, hsend, hrecv, asend, arecv, rsend, rrecv,
+    lsem, wsend, wrecv, fsend, frecv, hsend, hrecv, asend, arecv, rsend, rrecv,
 ):
     dp = lax.axis_index("dp")
     sp = lax.axis_index("space")
     core, yy, zh = dp % 2, (dp // 2) % NY, dp // (2 * NY)
     xx, zl = sp // NZ, sp % NZ
-    par, half = zl % 2, zl // 2
-    mine = 2 * xx + half
+    par, mine = zl // 2, 2 * xx + zl % 2
+    band = 2 * mine + par
+    home = sp // 2
+    traded = (zl == 1) | (zl == 2)
 
     def at(z_hi, y, c, x, z_lo):
         return {"dp": (z_hi * NY + y) * 2 + c, "space": x * NZ + z_lo}
@@ -50,15 +52,21 @@
     dev_mir = at(1 - zh, yy, core, xx, NZ - 1 - zl)
     dev_xup = at(zh, yy, core, (xx + 1) % NX, zl)
     dev_xdn = at(zh, yy, core, (xx + NX - 1) % NX, zl)
-    dev_next = {"dp": dp, "space": (sp + 1) % 16}
-    dev_prev = {"dp": dp, "space": (sp + 15) % 16}
+    dev_trade = at(zh, yy, core, xx, NZ - 1 - zl)
+    last_x, last_z = (xx + zl // 3) % NX, jnp.where(zl == 0, 2, jnp.where(zl == 2, 3, 0))
+    first_x, first_z = jnp.where(zl == 0, xx + NX - 1, xx) % NX, jnp.where(zl == 0, 3, jnp.where(zl == 3, 1, 0))
+    dev_last = at(zh, yy, core, last_x, last_z)
+    dev_first = at(zh, yy, core, first_x, first_z)
 
     def member(k):
-        return {"dp": dp, "space": (k // 2) * NZ + (k % 2) * 2 + par}
+        return {"dp": dp, "space": (k // 2) * NZ + 2 * par + k % 2}
+
+    def owner(k):
+        return {"dp": dp, "space": 2 * k + par}
 
     barrier = pltpu.get_barrier_semaphore()
-    peers = [dev_up, dev_dn, dev_far, dev_sib, dev_mir, dev_next, dev_prev]
-    peers += [member((mine + m) % 8) for m in range(1, 8)]
+    peers = [dev_up, dev_dn, dev_far, dev_sib, dev_mir]
+    peers += [{"dp": dp, "space": (sp + m) % 16} for m in range(1, 16)]
     for peer in peers:
         pl.semaphore_signal(barrier, inc=1, device_id=peer)
 
@@ -74,6 +82,13 @@
         copy.start()
         pending.append(copy)
 
+    guarded = []
+
+    def push_if(cond, src, dst, send, recv, dev):
+        copy = remote(src, dst, send, recv, dev)
+        pl.when(cond)(copy.start)
+        guarded.append((cond, copy))
+
     def shard(z_hi, y, c):
         return (z_hi * NY + y) * 2 + c
 
@@ -84,12 +99,19 @@
     loads = [
         pltpu.make_async_copy(wex_ref, we.at[own_d], lsem.at[0]),
         pltpu.make_async_copy(wpr_ref, w1.at[own_d], lsem.at[1]),
-        pltpu.make_async_copy(f_ref, fbuf, lsem.at[2]),
-        pltpu.make_async_copy(wqkv_ref, w2.at[own_d, 0:96], lsem.at[3]),
-        pltpu.make_async_copy(wout_ref, w2.at[own_d, 96:128], lsem.at[4]),
+        pltpu.make_async_copy(wqkv_ref, w2.at[own_d, 0:96], lsem.at[2]),
+        pltpu.make_async_copy(wout_ref, w2.at[own_d, 96:128], lsem.at[3]),
     ]
     for load in loads:
         load.start()
+
+    def pair(q):
+        return pl.ds(2 * q, 2)
+
+    stays = [(jnp.logical_not(traded), f_ref.at[pair(q)], fbuf.at[pair(q)], frecv.at[q]) for q in range(4)]
+    stays += [(zl == 1, f_ref.at[ROWS - 1], halo.at[0], hrecv.at[0]), (zl == 2, f_ref.at[0], halo.at[1], hrecv.at[1])]
+    for cond, src, dst, sem in stays:
+        pl.when(cond)(pltpu.make_async_copy(src, dst, sem).start)
     pl.semaphore_wait(barrier, len(peers))
 
     odd = xx % 2
@@ -146,8 +168,10 @@
 
     loads[0].wait()
     g_start(0)
-    push(f_ref.at[ROWS - 1], halo.at[0], hsend.at[0], hrecv.at[0], dev_next)
-    push(f_ref.at[0], halo.at[1], hsend.at[1], hrecv.at[1], dev_prev)
+    push_if(zl != 1, f_ref.at[ROWS - 1], halo.at[0], hsend.at[0], hrecv.at[0], dev_last)
+    for q in range(4):
+        push_if(traded, f_ref.at[pair(q)], fbuf.at[pair(q)], fsend.at[q], frecv.at[q], dev_trade)
+    push_if(zl != 2, f_ref.at[0], halo.at[1], hsend.at[1], hrecv.at[1], dev_first)
     loads[1].wait()
     g_start(1)
 
@@ -160,96 +184,72 @@
         xn[row] = (moved * bns_ref[...] + bnb_ref[...]).astype(BF16)
         return moved.astype(BF16)
 
-    loads[2].wait()
-
-    @pl.loop(0, ROWS)
-    def _(r):
-        fperm[r] = prep(r + 1, fbuf[r])
-
-    sub = lax.broadcasted_iota(jnp.int32, (2, 8, 128), 1)
-
-    def expanded(x, g):
+    def take(q):
+        remote(fbuf.at[pair(q)], fbuf.at[pair(q)], fsend.at[q], frecv.at[q], dev_trade).wait_recv()
+        for r in range(2 * q, 2 * q + 2):
+            fperm[r] = prep(r + 1, fbuf[r])
+
+    def expand_rows(first, count, g):
         w = jnp.concatenate([we[2 * g], we[2 * g + 1]], axis=1)
         bias = be_ref[:, pl.ds(pl.multiple_of(256 * g, 256), 256)]
-        return gelu(dot_nn(x, w) + bias)
-
-    def store(g, e, put):
+        rows = slice(first, first + count)
+        e = gelu(dot_nn(xn[rows].reshape(count * COLS, CH), w) + bias)
+        sub = lax.broadcasted_iota(jnp.int32, (count, 8, 128), 1)
         for k in range(2):
-            part = e[:, 128 * k : 128 * (k + 1)].reshape(2, 16, 8, 128)
-            before = jnp.where(sub == 0, 0.0, pltpu.roll(part[:, 15], 1, 1))
-            after = jnp.where(sub == 7, 0.0, pltpu.roll(part[:, 0], 7, 1))
-            put(2 * g + k, slice(1, 17), part)
-            put(2 * g + k, 0, before)
-            put(2 * g + k, 17, after)
-
-    def expand(i):
+            part = e[:, 128 * k : 128 * (k + 1)].reshape(count, 16, 8, 128)
+            ebuf[2 * g + k, rows, 1:17] = part
+            ebuf[2 * g + k, rows, 0] = jnp.where(sub == 0, 0.0, pltpu.roll(part[:, 15], 1, 1))
+            ebuf[2 * g + k, rows, 17] = jnp.where(sub == 7, 0.0, pltpu.roll(part[:, 0], 7, 1))
+
+    def early(i):
+        sib_wait(0, i)
         z_hi, y = places[i]
-        g = z_hi * NY + y
-
-        @pl.loop(0, ROWS // 2)
-        def _(r2):
-            rows = pl.ds(2 * r2 + 1, 2)
-
-            def put(l, b, value):
-                ebuf[l, rows, b] = value
-
-            store(g, expanded(xn[rows].reshape(2 * COLS, CH), g), put)
-
-    def expand_rim():
-        remote(halo.at[0], halo.at[0], hsend.at[0], hrecv.at[0], dev_next).wait_recv()
-        remote(halo.at[1], halo.at[1], hsend.at[1], hrecv.at[1], dev_prev).wait_recv()
-        prep(0, halo[0])
-        prep(ROWS + 1, halo[1])
+        expand_rows(1, 2, z_hi * NY + y)
+
+    def expand(q):
+        take(q)
 
         @pl.loop(0, 8)
         def _(g):
-            x = jnp.concatenate([xn[0], xn[ROWS + 1]], axis=0)
-
-            def put(l, b, value):
-                ebuf[l, 0, b] = value[0]
-                ebuf[l, ROWS + 1, b] = value[1]
-
-            store(g, expanded(x, g), put)
-
-        @pl.when(sp == 0)
+            expand_rows(2 * q + 1, 2, g)
+
+    def expand_rim(side):
+        remote(halo.at[side], halo.at[side], hsend.at[side], hrecv.at[side], dev_trade).wait_recv()
+        at_row = (ROWS + 1) * side
+        prep(at_row, halo[side])
+
+        @pl.loop(0, 8)
+        def _(g):
+            expand_rows(at_row, 1, g)
+
+        @pl.when(band == 15 * side)
         def _():
-            ebuf[:, 0] = jnp.zeros((16, 18, 8, 128), F32)
-
-        @pl.when(sp == 15)
-        def _():
-            ebuf[:, ROWS + 1] = jnp.zeros((16, 18, 8, 128), F32)
-
-    sib_wait(0, 7)
-    g_arrive(0, 1, 2, 3)
-    expand(7)
-    g_arrive(0, 0)
+            ebuf[:, at_row] = jnp.zeros((16, 18, 8, 128), F32)
+
+    g_arrive(0, 1, 2, 3, 0)
+    g_arrive(1, 1, 2, 3, 0)
+    take(0)
+    early(7)
     g_finish(0, 1, 2, 3)
-    sib_wait(0, 1)
+    early(1)
+    g_finish(0, 0)
+    early(2)
+    g_arrive(0, 4, 5, 6)
+    early(3)
+    g_finish(1, 1, 2, 3)
+    early(0)
+    g_finish(0, 4, 5, 6)
+    g_arrive(1, 4, 5, 6)
+    early(4)
+    g_finish(1, 0)
+    early(5)
+    early(6)
+    loads[2].wait()
+    loads[3].wait()
+    g_start(2)
     expand(1)
-    g_arrive(1, 1, 2, 3)
-    g_finish(0, 0)
-    sib_wait(0, 2)
-    expand(2)
-    g_arrive(1, 0)
-    sib_wait(0, 3)
-    expand(3)
-    g_arrive(0, 4, 5, 6)
-    sib_wait(0, 0)
-    expand(0)
-    g_finish(0, 4, 5, 6)
-    loads[3].wait()
-    loads[4].wait()
-    g_start(2)
-    g_finish(1, 1, 2, 3, 0)
-    sib_wait(0, 4)
-    expand(4)
-    g_arrive(1, 4, 5, 6)
-    sib_wait(0, 5)
-    expand(5)
-    sib_wait(0, 6)
-    expand(6)
     g_finish(1, 4, 5, 6)
-    expand_rim()
+    expand_rim(0)
 
     def conv(q):
         @pl.loop(0, 8)
@@ -330,56 +330,61 @@
             done = done + gbuf[2 * q + r].reshape(128, CH).astype(F32)
             fin[2 * q + r] = done.astype(BF16).reshape(8, 16, CH)
 
-    keeps = []
-
     def send_back(q):
         rows = pl.ds(2 * q, 2)
-        for m in range(1, 8):
+        for m in range(8):
             k = (mine + m) % 8
-            push(
-                fin.at[rows, k], o_ref.at[rows, group(mine)], rsend.at[q, m - 1], rrecv.at[q, m - 1], member(k)
-            )
-        keep = pltpu.make_async_copy(fin.at[rows, mine], o_ref.at[rows, group(mine)], lsem.at[5 + q])
-        keep.start()
-        keeps.append(keep)
+            src, dst = fin.at[rows, k], o_ref.at[rows, group(mine)]
+            if m == 0:
+                push_if(traded, src, dst, rsend.at[q, m], rrecv.at[q, m], owner(k))
+                keep = pltpu.make_async_copy(src, dst, rrecv.at[q, m])
+                pl.when(jnp.logical_not(traded))(keep.start)
+            else:
+                push(src, dst, rsend.at[q, m], rrecv.at[q, m], owner(k))
 
     def returned(q):
         rows = pl.ds(2 * q, 2)
-        for m in range(1, 8):
-            k = (mine + 8 - m) % 8
-            ref = o_ref.at[rows, group(k)]
-            remote(ref, ref, rsend.at[q, m - 1], rrecv.at[q, m - 1], member(k)).wait_recv()
+        for m in range(8):
+            ref = o_ref.at[rows, group((home + 8 - m) % 8)]
+            remote(ref, ref, rsend.at[q, m], rrecv.at[q, m], dev_trade).wait_recv()
 
     conv(0)
     sib_wait(1, *range(8))
     project(0)
     forward(0)
     g_arrive(2, 1, 2, 3, 0)
+    expand(2)
     conv(1)
     project(1)
     forward(1)
     g_arrive(2, 4, 5, 6)
     g_finish(2, 1, 2, 3, 0)
-    conv(2)
-    project(2)
-    forward(2)
+    expand(3)
     g_finish(2, 4, 5, 6)
     sib_wait(2, *range(8))
     arrived(0)
     attend(0)
     send_back(0)
+    expand_rim(1)
+    conv(2)
+    project(2)
+    forward(2)
+    arrived(1)
+    attend(1)
+    send_back(1)
     conv(3)
     project(3)
     forward(3)
-    for q in range(1, 4):
+    for q in range(2, 4):
         arrived(q)
         attend(q)
         send_back(q)
     for q in range(4):
-        keeps[q].wait()
         returned(q)
     for copy in pending:
         copy.wait_send()
+    for cond, copy in guarded:
+        pl.when(cond)(copy.wait_send)
 
 
 def local(
@@ -407,15 +412,17 @@
             pltpu.VMEM((ROWS, 8, 16, CH), BF16),
             pltpu.VMEM((256, 3 * CH), BF16),
             pltpu.VMEM((ROWS, 8, 16, CH), BF16),
-            dma((9,)),
+            dma((4,)),
             dma((3, 29)),
             dma((3, 29)),
+            dma((4,)),
+            dma((4,)),
             dma((2,)),
             dma((2,)),
             dma((4, 7)),
             dma((4, 7)),
-            dma((4, 7)),
-            dma((4, 7)),
+            dma((4, 8)),
+            dma((4, 8)),
         ],
         compiler_params=pltpu.CompilerParams(
             collective_id=0, has_side_effects=True, vmem_limit_bytes=60 * 1024 * 1024

time: 93.2 us -> 85.3 us (0.915); the launches traced: 93 us -> 84 us
  Pallas kernels: 90.5 us -> 81.4 us
    pallas_call x1, Pallas kernels: 90.5 us -> 81.4 us  [local(): pl.pallas_call(kernel, out_shape=jax.ShapeDtypeStruct((ROWS, COLS, CH), B...]
where the time goes in v3:
time: 85.3 us; the launch traced here: 84 us
  Pallas kernels  81.4 us (95%)
  local copies, waits for them, and re-layouts  2.55 us (3%)
    pallas_call x1, Pallas kernels, local(): pl.pallas_call(kernel, out_shape=jax.ShapeDtypeStruct((ROWS, COLS, CH), B...  81.4 us
    transpose x1, local copies, waits for them, and re-layouts, local(): out.reshape(ROWS, 16, 8, CH).transpose(0, 2, 1, 3).reshape(fields.shape)  2.55 us

profile of v3, /device:TPU:1, one launch (start us, length us, event | category | flops | bytes accessed | tf_op | source)
XLA Modules:
  0.0 84.0 jit_solution(9810328963898780327)
XLA Ops:
  0.0 81.4 %shard_map.118 = bf16[8,128,512]{2,1,0:T(8,128)(2,1)} custom-call(bf16[8,128,512]{2,1,0:T(8,128)(2,1)} %bitcast.15, f32[1,512]{1,0:T(1,128)} %bitcast.21, f32[1,512]{1,0:T(1,128)} %bitcast.22, bf16[512,128]{1,0:T(8,128)(2,1)} %wex_ref.1, f32[1,2048]{1,0:T(1,128)} %bitcast.19, f32[3,3,2048]{2,1,0:T(4,128)} %dwk_ref.1, f32[1,2048]{1,0:T(1,128)} %bitcast.20, ...), custom_call_target="tpu_custom_call" | custom-call | tf_op jit(solution)/shard_map/pallas_call | solution.py:396
  81.4 2.5 %copy.13 = bf16[8,8,16,512]{3,2,1,0:T(8,128)(2,1)} copy(bf16[8,8,16,512]{3,1,2,0:T(8,128)(2,1)} %bitcast.14) | data formatting | bytes 2097152 | tf_op jit(solution)/shard_map/transpose | solution.py:444

commit v4 on v3

--- a/solution.py
+++ b/solution.py
@@ -27,8 +27,9 @@
 
 
 def kernel(
-    f_ref, bns_ref, bnb_ref, wex_ref, be_ref, dwk_ref, dwb_ref, wpr_ref, lng_ref, lnb_ref, wqkv_ref, wout_ref,
+    f_ref, bns_in, bnb_in, wex_ref, be_in, dwk_in, dwb_in, wpr_ref, lng_in, lnb_in, wqkv_ref, wout_ref,
     o_ref,
+    bns_ref, bnb_ref, be_ref, dwk_ref, dwb_ref, lng_ref, lnb_ref,
     fbuf, halo, fperm, xn, we, w1, w2, ebuf, sbuf, co, gbuf, qkv, fin,
     lsem, wsend, wrecv, fsend, frecv, hsend, hrecv, asend, arecv, rsend, rrecv,
 ):
@@ -102,6 +103,11 @@
         pltpu.make_async_copy(wqkv_ref, w2.at[own_d, 0:96], lsem.at[2]),
         pltpu.make_async_copy(wout_ref, w2.at[own_d, 96:128], lsem.at[3]),
     ]
+    small = [
+        (bns_in, bns_ref), (bnb_in, bnb_ref), (be_in, be_ref), (dwk_in, dwk_ref),
+        (dwb_in, dwb_ref), (lng_in, lng_ref), (lnb_in, lnb_ref),
+    ]
+    loads += [pltpu.make_async_copy(src, dst, lsem.at[4 + n]) for n, (src, dst) in enumerate(small)]
     for load in loads:
         load.start()
 
@@ -189,38 +195,43 @@
         for r in range(2 * q, 2 * q + 2):
             fperm[r] = prep(r + 1, fbuf[r])
 
-    def expand_rows(first, count, g):
-        w = jnp.concatenate([we[2 * g], we[2 * g + 1]], axis=1)
-        bias = be_ref[:, pl.ds(pl.multiple_of(256 * g, 256), 256)]
-        rows = slice(first, first + count)
-        e = gelu(dot_nn(xn[rows].reshape(count * COLS, CH), w) + bias)
+    def expand_rows(first, count, *gs):
+        rows = pl.ds(first, count)
+        x = xn[rows].reshape(count * COLS, CH)
+        sums = [dot_nn(x, jnp.concatenate([we[2 * g], we[2 * g + 1]], axis=1)) for g in gs]
         sub = lax.broadcasted_iota(jnp.int32, (count, 8, 128), 1)
-        for k in range(2):
-            part = e[:, 128 * k : 128 * (k + 1)].reshape(count, 16, 8, 128)
-            ebuf[2 * g + k, rows, 1:17] = part
-            ebuf[2 * g + k, rows, 0] = jnp.where(sub == 0, 0.0, pltpu.roll(part[:, 15], 1, 1))
-            ebuf[2 * g + k, rows, 17] = jnp.where(sub == 7, 0.0, pltpu.roll(part[:, 0], 7, 1))
-
-    def early(i):
-        sib_wait(0, i)
-        z_hi, y = places[i]
-        expand_rows(1, 2, z_hi * NY + y)
+        for g, summed in zip(gs, sums):
+            e = gelu(summed + be_ref[:, pl.ds(pl.multiple_of(256 * g, 256), 256)])
+            for k in range(2):
+                part = e[:, 128 * k : 128 * (k + 1)].reshape(count, 16, 8, 128)
+                ebuf[2 * g + k, rows, 1:17] = part
+                ebuf[2 * g + k, rows, 0] = jnp.where(sub == 0, 0.0, pltpu.roll(part[:, 15], 1, 1))
+                ebuf[2 * g + k, rows, 17] = jnp.where(sub == 7, 0.0, pltpu.roll(part[:, 0], 7, 1))
+
+    def early(*which):
+        sib_wait(0, *which)
+        for i in which:
+            z_hi, y = places[i]
+
+            @pl.loop(0, 2)
+            def _(q):
+                expand_rows(2 * q + 1, 2, z_hi * NY + y)
 
     def expand(q):
         take(q)
 
-        @pl.loop(0, 8)
+        @pl.loop(0, 4)
         def _(g):
-            expand_rows(2 * q + 1, 2, g)
+            expand_rows(2 * q + 1, 2, 2 * g, 2 * g + 1)
 
     def expand_rim(side):
         remote(halo.at[side], halo.at[side], hsend.at[side], hrecv.at[side], dev_trade).wait_recv()
         at_row = (ROWS + 1) * side
         prep(at_row, halo[side])
 
-        @pl.loop(0, 8)
+        @pl.loop(0, 4)
         def _(g):
-            expand_rows(at_row, 1, g)
+            expand_rows(at_row, 1, 2 * g, 2 * g + 1)
 
         @pl.when(band == 15 * side)
         def _():
@@ -228,44 +239,38 @@
 
     g_arrive(0, 1, 2, 3, 0)
     g_arrive(1, 1, 2, 3, 0)
-    take(0)
-    early(7)
-    g_finish(0, 1, 2, 3)
-    early(1)
-    g_finish(0, 0)
-    early(2)
-    g_arrive(0, 4, 5, 6)
-    early(3)
-    g_finish(1, 1, 2, 3)
-    early(0)
-    g_finish(0, 4, 5, 6)
-    g_arrive(1, 4, 5, 6)
-    early(4)
-    g_finish(1, 0)
-    early(5)
-    early(6)
     loads[2].wait()
     loads[3].wait()
     g_start(2)
-    expand(1)
+    for load in loads[4:]:
+        load.wait()
+    take(0)
+    g_finish(0, 1, 2, 3, 0)
+    g_arrive(0, 4, 5, 6)
+    take(1)
+    g_finish(1, 1, 2, 3, 0)
+    early(7, 1)
+    g_finish(0, 4, 5, 6)
+    g_arrive(1, 4, 5, 6)
+    early(2, 3, 0)
     g_finish(1, 4, 5, 6)
+    early(4, 5, 6)
+    g_arrive(2, 1, 2, 3, 0)
     expand_rim(0)
 
-    def conv(q):
-        @pl.loop(0, 8)
-        def _(g):
-            for k in range(2):
-                lanes = pl.ds(pl.multiple_of(256 * g + 128 * k, 128), 128)
-                bias = dwb_ref[:, lanes]
-                for r in range(2):
-                    acc = jnp.broadcast_to(bias[None], (16, 8, 128))
-                    for i in range(3):
-                        for j in range(3):
-                            tap = dwk_ref[i, j : j + 1, lanes]
-                            acc = acc + ebuf[2 * g + k, 2 * q + r + i, j : j + 16] * tap[None]
-                    sbuf[g, 128 * r : 128 * (r + 1), 128 * k : 128 * (k + 1)] = (
-                        gelu(acc).astype(BF16).reshape(128, 128)
-                    )
+    def conv(q, g):
+        for k in range(2):
+            lanes = pl.ds(pl.multiple_of(256 * g + 128 * k, 128), 128)
+            bias = dwb_ref[:, lanes]
+            for r in range(2):
+                summed = jnp.broadcast_to(bias[None], (16, 8, 128))
+                for i in range(3):
+                    for j in range(3):
+                        tap = dwk_ref[i, j : j + 1, lanes]
+                        summed = summed + ebuf[2 * g + k, 2 * q + r + i, j : j + 16] * tap[None]
+                sbuf[g, 128 * r : 128 * (r + 1), 128 * k : 128 * (k + 1)] = (
+                    gelu(summed).astype(BF16).reshape(128, 128)
+                )
 
     def project(q):
         w = w1[...].reshape(CH, FF)
@@ -273,6 +278,15 @@
         for g in range(8):
             total = total + dot_nt(sbuf[g], w[:, 256 * g : 256 * (g + 1)])
         co[2 * q : 2 * q + 2] = total.astype(BF16).reshape(2, COLS, CH)
+
+    def mbconv(q):
+        @pl.loop(0, 8)
+        def _(g):
+            conv(q, g)
+
+        if q == 0:
+            sib_wait(1, *range(8))
+        project(q)
 
     def group(k):
         return pl.ds(pl.multiple_of(16 * k, 16), 16)
@@ -348,32 +362,26 @@
             ref = o_ref.at[rows, group((home + 8 - m) % 8)]
             remote(ref, ref, rsend.at[q, m], rrecv.at[q, m], dev_trade).wait_recv()
 
-    conv(0)
-    sib_wait(1, *range(8))
-    project(0)
+    mbconv(0)
     forward(0)
-    g_arrive(2, 1, 2, 3, 0)
+    g_finish(2, 1, 2, 3, 0)
+    g_arrive(2, 4, 5, 6)
     expand(2)
-    conv(1)
-    project(1)
+    mbconv(1)
     forward(1)
-    g_arrive(2, 4, 5, 6)
-    g_finish(2, 1, 2, 3, 0)
+    g_finish(2, 4, 5, 6)
     expand(3)
-    g_finish(2, 4, 5, 6)
     sib_wait(2, *range(8))
     arrived(0)
     attend(0)
     send_back(0)
     expand_rim(1)
-    conv(2)
-    project(2)
+    mbconv(2)
     forward(2)
     arrived(1)
     attend(1)
     send_back(1)
-    conv(3)
-    project(3)
+    mbconv(3)
     forward(3)
     for q in range(2, 4):
         arrived(q)
@@ -390,15 +398,21 @@
 def local(
     fields, bn_scale, bn_shift, w_expand, expand_bias, dw_kernel, dw_bias, w_project, ln_gain, ln_bias, w_qkv, w_out
 ):
-    vmem = pl.BlockSpec(memory_space=pltpu.VMEM)
     hbm = pl.BlockSpec(memory_space=pl.ANY)
     dma = pltpu.SemaphoreType.DMA
     out = pl.pallas_call(
         kernel,
         out_shape=jax.ShapeDtypeStruct((ROWS, COLS, CH), BF16),
-        in_specs=[hbm, vmem, vmem, hbm, vmem, vmem, vmem, hbm, vmem, vmem, hbm, hbm],
+        in_specs=[hbm] * 12,
         out_specs=hbm,
         scratch_shapes=[
+            pltpu.VMEM((1, CH), F32),
+            pltpu.VMEM((1, CH), F32),
+            pltpu.VMEM((1, FF), F32),
+            pltpu.VMEM((3, 3, FF), F32),
+            pltpu.VMEM((1, FF), F32),
+            pltpu.VMEM((1, CH), F32),
+            pltpu.VMEM((1, CH), F32),
             pltpu.VMEM((ROWS, COLS, CH), BF16),
             pltpu.VMEM((2, COLS, CH), BF16),
             pltpu.VMEM((ROWS, COLS, CH), BF16),
@@ -412,7 +426,7 @@
             pltpu.VMEM((ROWS, 8, 16, CH), BF16),
             pltpu.VMEM((256, 3 * CH), BF16),
             pltpu.VMEM((ROWS, 8, 16, CH), BF16),
-            dma((4,)),
+            dma((11,)),
             dma((3, 29)),
             dma((3, 29)),
             dma((4,)),

time: 85.3 us -> 79.9 us (0.937)
  Pallas kernels: 81.4 us -> 76 us
    pallas_call x1, Pallas kernels: 81.4 us -> 76 us  [local(): pl.pallas_call(kernel, out_shape=jax.ShapeDtypeStruct((ROWS, COLS, CH), B...]
where the time goes in v4:
time: 79.9 us; the launch traced here: 78.6 us
  Pallas kernels  76 us (95%)
  local copies, waits for them, and re-layouts  2.55 us (3%)
    pallas_call x1, Pallas kernels, local(): pl.pallas_call(kernel, out_shape=jax.ShapeDtypeStruct((ROWS, COLS, CH), B...  76 us
    transpose x1, local copies, waits for them, and re-layouts, local(): out.reshape(ROWS, 16, 8, CH).transpose(0, 2, 1, 3).reshape(fields.shape)  2.55 us

profile of v4, /device:TPU:1, one launch (start us, length us, event | category | flops | bytes accessed | tf_op | source)
XLA Modules:
  0.0 78.6 jit_solution(4093728048019888491)
XLA Ops:
  0.0 76.0 %shard_map.118 = bf16[8,128,512]{2,1,0:T(8,128)(2,1)} custom-call(bf16[8,128,512]{2,1,0:T(8,128)(2,1)} %bitcast.15, f32[1,512]{1,0:T(1,128)} %bitcast.21, f32[1,512]{1,0:T(1,128)} %bitcast.22, bf16[512,128]{1,0:T(8,128)(2,1)} %wex_ref.1, f32[1,2048]{1,0:T(1,128)} %bitcast.19, f32[3,3,2048]{2,1,0:T(4,128)} %dwk_in.1, f32[1,2048]{1,0:T(1,128)} %bitcast.20, ...), custom_call_target="tpu_custom_call" | custom-call | tf_op jit(solution)/shard_map/pallas_call | solution.py:403
  76.0 2.5 %copy.13 = bf16[8,8,16,512]{3,2,1,0:T(8,128)(2,1)} copy(bf16[8,8,16,512]{3,1,2,0:T(8,128)(2,1)} %bitcast.14) | data formatting | bytes 2097152 | tf_op jit(solution)/shard_map/transpose | solution.py:458

commit v5 on v4

--- a/solution.py
+++ b/solution.py
@@ -10,6 +10,8 @@
 NY, NX, NZ = 4, 4, 4
 ROWS, COLS, CH, FF = 8, 128, 512, 2048
 Q_SCALE = 1.4426950408889634 / (32.0**0.5)
+V_SCALE = 2.0**-10
+TOP = float(jnp.finfo(jnp.bfloat16).max)
 
 
 def dot_nn(a, b):
@@ -20,10 +22,8 @@
     return lax.dot_general(a, b, (((1,), (1,)), ((), ())), preferred_element_type=F32)
 
 
-def gelu(x):
-    inner = x * (0.7978845608028654 + 0.035677408136300125 * (x * x))
-    half = 0.5 * x
-    return half + half * jnp.tanh(inner)
+def twice_gelu(x):
+    return x + x * jnp.tanh(x * (0.7978845608028654 + 0.035677408136300125 * (x * x)))
 
 
 def kernel(
@@ -138,7 +138,8 @@
         remote(ref, ref, wsend.at[ph, slot], wrecv.at[ph, slot], dev_sib).wait_recv()
 
     def carried(ph, i):
-        return piece(ph, shard(*places[i], core), 2 * odd, 2)
+        d = shard(*places[i], core)
+        return bufs[ph].at[d] if ph == 2 else piece(ph, d, 2 * odd, 2)
 
     def spread(ph, i, base):
         ref = carried(ph, i)
@@ -157,6 +158,9 @@
             if i == 0:
                 spread(ph, 0, 4)
             d = shard(*places[i], core)
+            if ph == 2:
+                wpush(ph, 22 + i, bufs[ph].at[d], dev_sib)
+                continue
             wpush(ph, 7 + 2 * i, piece(ph, d, 2 * odd, 1), dev_xup)
             wpush(ph, 8 + 2 * i, piece(ph, d, 2 * odd + 1, 1), dev_xdn)
 
@@ -201,7 +205,7 @@
         sums = [dot_nn(x, jnp.concatenate([we[2 * g], we[2 * g + 1]], axis=1)) for g in gs]
         sub = lax.broadcasted_iota(jnp.int32, (count, 8, 128), 1)
         for g, summed in zip(gs, sums):
-            e = gelu(summed + be_ref[:, pl.ds(pl.multiple_of(256 * g, 256), 256)])
+            e = twice_gelu(summed + be_ref[:, pl.ds(pl.multiple_of(256 * g, 256), 256)])
             for k in range(2):
                 part = e[:, 128 * k : 128 * (k + 1)].reshape(count, 16, 8, 128)
                 ebuf[2 * g + k, rows, 1:17] = part
@@ -244,6 +248,7 @@
     g_start(2)
     for load in loads[4:]:
         load.wait()
+    dwk_ref[...] = 0.5 * dwk_ref[...]
     take(0)
     g_finish(0, 1, 2, 3, 0)
     g_arrive(0, 4, 5, 6)
@@ -253,9 +258,10 @@
     g_finish(0, 4, 5, 6)
     g_arrive(1, 4, 5, 6)
     early(2, 3, 0)
+    g_arrive(2, 0)
     g_finish(1, 4, 5, 6)
     early(4, 5, 6)
-    g_arrive(2, 1, 2, 3, 0)
+    g_arrive(2, 1, 2, 3)
     expand_rim(0)
 
     def conv(q, g):
@@ -269,14 +275,15 @@
                         tap = dwk_ref[i, j : j + 1, lanes]
                         summed = summed + ebuf[2 * g + k, 2 * q + r + i, j : j + 16] * tap[None]
                 sbuf[g, 128 * r : 128 * (r + 1), 128 * k : 128 * (k + 1)] = (
-                    gelu(summed).astype(BF16).reshape(128, 128)
+                    twice_gelu(summed).astype(BF16).reshape(128, 128)
                 )
 
     def project(q):
         w = w1[...].reshape(CH, FF)
-        total = fperm[2 * q : 2 * q + 2].reshape(2 * COLS, CH).astype(F32)
-        for g in range(8):
+        total = dot_nt(sbuf[0], w[:, 0:256])
+        for g in range(1, 8):
             total = total + dot_nt(sbuf[g], w[:, 256 * g : 256 * (g + 1)])
+        total = 0.5 * total + fperm[2 * q : 2 * q + 2].reshape(2 * COLS, CH).astype(F32)
         co[2 * q : 2 * q + 2] = total.astype(BF16).reshape(2, COLS, CH)
 
     def mbconv(q):
@@ -312,6 +319,7 @@
     heads = [(lane // 32 == n) for n in range(4)]
     same = (lane // 8) % 2 == (row // 8) % 2
     same4 = jnp.concatenate([same] * 4, axis=0)
+    ones = jnp.concatenate([m.astype(BF16) for m in heads], axis=0)
 
     def attend(q):
         held = gbuf[2 * q : 2 * q + 2].reshape(256, CH).astype(F32)
@@ -322,73 +330,66 @@
         w = w2[:, 0:96].reshape(3 * CH, CH)
         qkv[:, 0:CH] = (dot_nt(ln, w[0:CH]) * Q_SCALE).astype(BF16)
         qkv[:, CH : 2 * CH] = dot_nt(ln, w[CH : 2 * CH]).astype(BF16)
-        qkv[:, 2 * CH :] = dot_nt(ln, w[2 * CH :]).astype(BF16)
-
-        @pl.loop(0, 2)
-        def _(r):
-            rows = pl.ds(pl.multiple_of(128 * r, 128), 128)
+        qkv[:, 2 * CH :] = (dot_nt(ln, w[2 * CH :]) * V_SCALE).astype(BF16)
+
+        for r in range(2):
             parts = []
             for gr in range(4):
                 lo = 128 * gr
+                rows = slice(128 * r, 128 * (r + 1))
                 qv = qkv[rows, lo : lo + 128]
                 kv = qkv[rows, CH + lo : CH + lo + 128]
                 vv = qkv[rows, 2 * CH + lo : 2 * CH + lo + 128]
                 zero = jnp.zeros_like(qv)
                 qm = jnp.concatenate([jnp.where(m, qv, zero) for m in heads], axis=0)
                 vm = jnp.concatenate([jnp.where(m, vv, zero) for m in heads], axis=0)
-                e = jnp.where(same4, jnp.exp2(dot_nt(qm, kv)), 0.0)
-                p = (e * (1.0 / jnp.sum(e, axis=1, keepdims=True))).astype(BF16)
-                wide = jnp.concatenate([p[128 * n : 128 * (n + 1)] for n in range(4)], axis=1)
-                parts.append(dot_nn(wide, vm).astype(BF16))
+                e = jnp.where(same4, jnp.minimum(jnp.exp2(dot_nt(qm, kv)), TOP), 0.0).astype(BF16)
+                wide = jnp.concatenate([e[128 * n : 128 * (n + 1)] for n in range(4)], axis=1)
+                both = dot_nn(wide, jnp.concatenate([vm, ones], axis=1))
+                parts.append((both[:, 0:128] * (1.0 / both[:, 128:]) * (1.0 / V_SCALE)).astype(BF16))
             done = dot_nt(jnp.concatenate(parts, axis=1), w2[:, 96:128].reshape(CH, CH))
             done = done + gbuf[2 * q + r].reshape(128, CH).astype(F32)
             fin[2 * q + r] = done.astype(BF16).reshape(8, 16, CH)
-
-    def send_back(q):
-        rows = pl.ds(2 * q, 2)
+            send_back(2 * q + r)
+
+    def send_back(r):
         for m in range(8):
             k = (mine + m) % 8
-            src, dst = fin.at[rows, k], o_ref.at[rows, group(mine)]
+            src, dst = fin.at[r, k], o_ref.at[r, group(mine)]
             if m == 0:
-                push_if(traded, src, dst, rsend.at[q, m], rrecv.at[q, m], owner(k))
-                keep = pltpu.make_async_copy(src, dst, rrecv.at[q, m])
+                push_if(traded, src, dst, rsend.at[r, m], rrecv.at[r, m], owner(k))
+                keep = pltpu.make_async_copy(src, dst, rrecv.at[r, m])
                 pl.when(jnp.logical_not(traded))(keep.start)
             else:
-                push(src, dst, rsend.at[q, m], rrecv.at[q, m], owner(k))
-
-    def returned(q):
-        rows = pl.ds(2 * q, 2)
+                push(src, dst, rsend.at[r, m], rrecv.at[r, m], owner(k))
+
+    def returned(r):
         for m in range(8):
-            ref = o_ref.at[rows, group((home + 8 - m) % 8)]
-            remote(ref, ref, rsend.at[q, m], rrecv.at[q, m], dev_trade).wait_recv()
+            ref = o_ref.at[r, group((home + 8 - m) % 8)]
+            remote(ref, ref, rsend.at[r, m], rrecv.at[r, m], dev_trade).wait_recv()
 
     mbconv(0)
     forward(0)
-    g_finish(2, 1, 2, 3, 0)
+    expand(2)
     g_arrive(2, 4, 5, 6)
-    expand(2)
     mbconv(1)
     forward(1)
-    g_finish(2, 4, 5, 6)
-    expand(3)
     sib_wait(2, *range(8))
     arrived(0)
     attend(0)
-    send_back(0)
-    expand_rim(1)
+    expand(3)
     mbconv(2)
     forward(2)
     arrived(1)
     attend(1)
-    send_back(1)
+    expand_rim(1)
     mbconv(3)
     forward(3)
     for q in range(2, 4):
         arrived(q)
         attend(q)
-        send_back(q)
-    for q in range(4):
-        returned(q)
+    for r in range(ROWS):
+        returned(r)
     for copy in pending:
         copy.wait_send()
     for cond, copy in guarded:
@@ -435,8 +436,8 @@
             dma((2,)),
             dma((4, 7)),
             dma((4, 7)),
-            dma((4, 8)),
-            dma((4, 8)),
+            dma((ROWS, 8)),
+            dma((ROWS, 8)),
         ],
         compiler_params=pltpu.CompilerParams(
             collective_id=0, has_side_effects=True, vmem_limit_bytes=60 * 1024 * 1024

time: 79.9 us -> 75.1 us (0.940)
  Pallas kernels: 76 us -> 71.9 us
    pallas_call x1, Pallas kernels: 76 us -> 71.9 us  [local(): pl.pallas_call(kernel, out_shape=jax.ShapeDtypeStruct((ROWS, COLS, CH), B...]
where the time goes in v5:
time: 75.1 us; the launch traced here: 74.4 us
  Pallas kernels  71.9 us (96%)
  local copies, waits for them, and re-layouts  2.55 us (3%)
    pallas_call x1, Pallas kernels, local(): pl.pallas_call(kernel, out_shape=jax.ShapeDtypeStruct((ROWS, COLS, CH), B...  71.9 us
    transpose x1, local copies, waits for them, and re-layouts, local(): out.reshape(ROWS, 16, 8, CH).transpose(0, 2, 1, 3).reshape(fields.shape)  2.55 us

profile of v5, /device:TPU:1, one launch (start us, length us, event | category | flops | bytes accessed | tf_op | source)
XLA Modules:
  0.0 74.4 jit_solution(1431724175917916863)
XLA Ops:
  0.0 71.9 %shard_map.118 = bf16[8,128,512]{2,1,0:T(8,128)(2,1)} custom-call(bf16[8,128,512]{2,1,0:T(8,128)(2,1)} %bitcast.15, f32[1,512]{1,0:T(1,128)} %bitcast.21, f32[1,512]{1,0:T(1,128)} %bitcast.22, bf16[512,128]{1,0:T(8,128)(2,1)} %wex_ref.1, f32[1,2048]{1,0:T(1,128)} %bitcast.19, f32[3,3,2048]{2,1,0:T(4,128)} %dwk_in.1, f32[1,2048]{1,0:T(1,128)} %bitcast.20, ...), custom_call_target="tpu_custom_call" | custom-call | tf_op jit(solution)/shard_map/pallas_call | solution.py:404
  71.9 2.5 %copy.13 = bf16[8,8,16,512]{3,2,1,0:T(8,128)(2,1)} copy(bf16[8,8,16,512]{3,1,2,0:T(8,128)(2,1)} %bitcast.14) | data formatting | bytes 2097152 | tf_op jit(solution)/shard_map/transpose | solution.py:459

commit v6 on v5

--- a/solution.py
+++ b/solution.py
@@ -252,12 +252,11 @@
     take(0)
     g_finish(0, 1, 2, 3, 0)
     g_arrive(0, 4, 5, 6)
-    take(1)
     g_finish(1, 1, 2, 3, 0)
-    early(7, 1)
     g_finish(0, 4, 5, 6)
     g_arrive(1, 4, 5, 6)
-    early(2, 3, 0)
+    take(1)
+    early(7, 1, 2, 3, 0)
     g_arrive(2, 0)
     g_finish(1, 4, 5, 6)
     early(4, 5, 6)

time: 75.1 us -> 74 us (0.985)
  the two profiles are of different devices: /device:TPU:1 before, /device:TPU:32 now
where the time goes in v6:
time: 74 us; the launch traced here: 73.9 us
  Pallas kernels  71.3 us (96%)
  local copies, waits for them, and re-layouts  2.55 us (3%)
    pallas_call x1, Pallas kernels, local(): pl.pallas_call(kernel, out_shape=jax.ShapeDtypeStruct((ROWS, COLS, CH), B...  71.3 us
    transpose x1, local copies, waits for them, and re-layouts, local(): out.reshape(ROWS, 16, 8, CH).transpose(0, 2, 1, 3).reshape(fields.shape)  2.55 us

profile of v6, /device:TPU:32, one launch (start us, length us, event | category | flops | bytes accessed | tf_op | source)
XLA Modules:
  0.0 73.9 jit_solution(5370189510882550456)
XLA Ops:
  0.0 71.3 %shard_map.118 = bf16[8,128,512]{2,1,0:T(8,128)(2,1)} custom-call(bf16[8,128,512]{2,1,0:T(8,128)(2,1)} %bitcast.15, f32[1,512]{1,0:T(1,128)} %bitcast.21, f32[1,512]{1,0:T(1,128)} %bitcast.22, bf16[512,128]{1,0:T(8,128)(2,1)} %wex_ref.1, f32[1,2048]{1,0:T(1,128)} %bitcast.19, f32[3,3,2048]{2,1,0:T(4,128)} %dwk_in.1, f32[1,2048]{1,0:T(1,128)} %bitcast.20, ...), custom_call_target="tpu_custom_call" | custom-call | tf_op jit(solution)/shard_map/pallas_call | solution.py:403
  71.3 2.5 %copy.13 = bf16[8,8,16,512]{3,2,1,0:T(8,128)(2,1)} copy(bf16[8,8,16,512]{3,1,2,0:T(8,128)(2,1)} %bitcast.14) | data formatting | bytes 2097152 | tf_op jit(solution)/shard_map/transpose | solution.py:458
